TPU v7x, 768 devices: a whole 4x8x12 slice. The times are simulated.
768 devices in a mesh: seq: 64 (over y, x, core), head: 12 (over z).
Axes of the slice: x: 4, y: 8, z: 12, core: 2. Of those that a mesh axis runs over, the one named last changes fastest.
Arguments:
- query_rows: bfloat16 [32768, 6144], P('seq', 'head'), may hold values from -6 to 6
- key_rows: bfloat16 [32768, 384], P('seq'), may hold values from -6 to 6
- value_rows: bfloat16 [32768, 384], P('seq'), may hold values from -6 to 6
- output_grad: bfloat16 [32768, 6144], P('seq', 'head'), may hold values from -0.59765625 to 0.59765625
- log_norm: float32 [48, 32768], P('head', 'seq'), may hold values from 0.5 to 3
- row_delta: float32 [48, 32768], P('head', 'seq'), may hold values from -5 to 5
- dispatch: int32 [64, 64], replicated, may hold values from 0 to 63, as said below
- listed_spans: int32 [64, 16], replicated, may hold values from 0 to 1023, as said below
- range_start: int32 [64, 64], replicated, may hold values from 0 to 32760, as said below
Outputs:
- query_grad: bfloat16 [32768, 6144], P('seq', 'head')
- key_grad: float32 [384, 32768], P('head', 'seq')
- value_grad: float32 [384, 32768], P('head', 'seq')
Inputs may be any that keep to these rules, and one draw needn't show every extreme that they name: `dispatch`: entry [h, j] names the group of query span 64 * h + j. Every group holds exactly 64 spans, and each row gives at most 1 spans to any one group, a number that every row reaches. `listed_spans`: row g holds 16 distinct key spans for group g. At most 1 of them lie among the 16 key spans of one index of seq, and every row reaches that number. `range_start`: entry [h, j] is at most 8 * (64 * h + j).
All inputs are finite; a program needn't handle non-finite values.
Results may differ from a plain program's by a relative error of at most 0.0046.
Values may be sent and summed in bfloat16 or wider, within the bound.
No kernel may reach another device: no remote copies, remote signals or barrier semaphores. Data moves between devices by JAX's collectives and lax.ppermute only.
A program may use at most 32 MiB of HBM per device.

v0:
```python
import math

import jax
import jax.numpy as jnp
from jax import lax
from jax.sharding import PartitionSpec as P

HD = 128
GROUP = 16
HQ_DEV = 4
SPAN = 8
KVCH = 32
NLIST = 16


HIGH = lax.Precision.HIGHEST


def sent_together(arrays, axis, split_dim, concat_dim, along):
    widths = [math.prod(a.shape[along:]) for a in arrays]
    both = jnp.concatenate(
        [a.reshape(*a.shape[:along], w) for a, w in zip(arrays, widths)], axis=along
    )
    whole = lax.all_to_all(both, axis, split_axis=split_dim, concat_axis=concat_dim, tiled=True)
    pieces = jnp.split(whole, [sum(widths[:k]) for k in range(1, len(widths))], axis=along)
    return tuple(
        (b.reshape(*whole.shape[:along], *a.shape[along:]) for a, b in zip(arrays, pieces))
    )


def sent_together_2(arrays, axis, split_dim, concat_dim, along):
    widths = [a.shape[along] for a in arrays]
    both = jnp.concatenate(arrays, axis=along)
    whole = lax.all_to_all(both, axis, split_axis=split_dim, concat_axis=concat_dim, tiled=True)
    return tuple(jnp.split(whole, [sum(widths[:k]) for k in range(1, len(widths))], axis=along))


def passed_along(value, axis, by):
    length = lax.axis_size(axis)
    pairs = [(i, i + by) for i in range(length) if 0 <= i + by < length]
    return lax.ppermute(value, axis, pairs)


def earlier_same(labels):
    count = labels.shape[-1]
    same = labels[..., :, None] == labels[..., None, :]
    before = jnp.arange(count)[:, None] > jnp.arange(count)[None, :]
    return jnp.sum(same & before, axis=-1)


def one_hot(index, count):
    return (index[..., None] == jnp.arange(count, dtype=jnp.int32)).astype(jnp.float32)


def group_total(stacked, members, position, from_after):
    share = stacked.shape[1] // members

    def block(index):
        return lax.dynamic_slice_in_dim(stacked, index * share, share, 1)

    running = block((position + 1) % members)
    for step in range(1, members):
        running = from_after(running) + block((position + 1 + step) % members)
    return running


def local(
    query_rows,
    key_rows,
    value_rows,
    output_grad,
    log_norm,
    row_delta,
    dispatch,
    listed_spans,
    range_start,
):
    owners = lax.axis_size("seq")
    home_index = lax.axis_index("seq")
    head_index = lax.axis_index("head")
    spans = dispatch.shape[1]
    slot_count = max(1, spans // owners)
    kv_count = max(1, NLIST // owners)
    tok_dev = query_rows.shape[0]
    width = query_rows.shape[1]
    heads = width // HD
    blocks = tok_dev // KVCH
    members = GROUP // heads
    position = head_index % members
    kv_head = head_index * heads // GROUP
    score_scale = 1.0 / math.sqrt(HD)
    rank_all = earlier_same(dispatch)
    slot_all = dispatch * slot_count + rank_all
    to_slot = one_hot(slot_all[home_index], owners * slot_count)
    to_slot_bf = to_slot.astype(jnp.bfloat16)
    pick_bf = to_slot.T.astype(jnp.bfloat16)
    pick_float = to_slot.T

    def send_rows(rows):
        return (
            jnp.dot(pick_bf, rows.reshape(spans, -1), preferred_element_type=jnp.float32)
            .astype(jnp.bfloat16)
            .reshape(owners, slot_count * SPAN, -1)
        )

    def send_stats(stats):
        placed = jnp.dot(pick_float, stats.T.reshape(spans, SPAN * heads), precision=HIGH)
        return placed.reshape(owners, slot_count * SPAN, heads)

    list_home = listed_spans // blocks
    list_sub = listed_spans % blocks
    list_rank = earlier_same(list_home)
    mine = (list_home == home_index).astype(jnp.float32)
    rank_hot = one_hot(list_rank, kv_count) * mine[..., None]
    sub_hot = one_hot(list_sub, blocks)
    select = jnp.einsum("nir,nim->nrm", rank_hot, sub_hot, precision=HIGH).reshape(
        owners * kv_count, blocks
    )
    select_bf = select.astype(jnp.bfloat16)
    key_head = lax.dynamic_slice_in_dim(key_rows, kv_head * HD, HD, 1)
    value_head = lax.dynamic_slice_in_dim(value_rows, kv_head * HD, HD, 1)

    def send_blocks(rows):
        placed = jnp.dot(
            select_bf, rows.reshape(blocks, KVCH * HD), preferred_element_type=jnp.float32
        )
        return placed.astype(jnp.bfloat16).reshape(owners, kv_count * KVCH, HD)

    query_got, grad_got, key_got, value_got = sent_together(
        (
            send_rows(query_rows),
            send_rows(output_grad),
            send_blocks(key_head),
            send_blocks(value_head),
        ),
        "seq",
        0,
        0,
        1,
    )
    norm_got, delta_got = sent_together_2(
        (send_stats(log_norm), send_stats(row_delta)), "seq", 0, 0, 1
    )
    live = (dispatch == home_index).reshape(-1)
    placement = jnp.cumsum(live.astype(jnp.int32)) - 1
    taken = live[:, None] & (placement[:, None] == jnp.arange(spans, dtype=jnp.int32)[None, :])
    source_slot = (jnp.arange(owners, dtype=jnp.int32)[:, None] * slot_count + rank_all).reshape(-1)
    compact = jnp.dot(
        taken.astype(jnp.float32).T, one_hot(source_slot, owners * slot_count), precision=HIGH
    )
    compact_bf = compact.astype(jnp.bfloat16)
    compact_back = compact.T.astype(jnp.bfloat16)
    flat_ids = jnp.arange(owners * spans, dtype=jnp.int32)
    span_ids = jnp.sum(jnp.where(taken, flat_ids[:, None], 0), axis=0)
    span_starts = jnp.sum(jnp.where(taken, range_start.reshape(-1)[:, None], 0), axis=0)

    def gather_rows(got):
        rows = jnp.dot(
            compact_bf, got.reshape(owners * slot_count, -1), preferred_element_type=jnp.float32
        )
        return rows.astype(jnp.bfloat16).reshape(spans * SPAN, heads, HD)

    def gather_stats(got):
        rows = jnp.dot(compact, got.reshape(owners * slot_count, SPAN * heads), precision=HIGH)
        return rows.reshape(spans * SPAN, heads).T

    query_mine = gather_rows(query_got)
    grad_mine = gather_rows(grad_got)
    norm_mine = gather_stats(norm_got)
    delta_mine = gather_stats(delta_got)
    my_list = listed_spans[home_index]
    kv_compact = one_hot(
        list_home[home_index] * kv_count + list_rank[home_index], owners * kv_count
    )
    kv_compact_bf = kv_compact.astype(jnp.bfloat16)

    def gather_blocks(got):
        rows = jnp.dot(
            kv_compact_bf,
            got.reshape(owners * kv_count, KVCH * HD),
            preferred_element_type=jnp.float32,
        )
        return rows.astype(jnp.bfloat16).reshape(NLIST * KVCH, HD)

    key_mine = gather_blocks(key_got)
    value_mine = gather_blocks(value_got)
    query_pos = (span_ids[:, None] * SPAN + jnp.arange(SPAN, dtype=jnp.int32)[None, :]).reshape(-1)
    key_pos = (my_list[:, None] * KVCH + jnp.arange(KVCH, dtype=jnp.int32)[None, :]).reshape(-1)
    lowest = jnp.repeat(span_starts, SPAN)
    allowed = (key_pos[None, :] <= query_pos[:, None]) & (key_pos[None, :] >= lowest[:, None])
    scores = (
        jnp.einsum("qhd,kd->hqk", query_mine, key_mine, preferred_element_type=jnp.float32)
        * score_scale
    )
    probs = jnp.where(allowed[None], jnp.exp(scores - norm_mine[:, :, None]), 0.0)
    dprobs = jnp.einsum("qhd,kd->hqk", grad_mine, value_mine, preferred_element_type=jnp.float32)
    dscores = probs * (dprobs - delta_mine[:, :, None])
    probs_bf = probs.astype(jnp.bfloat16)
    dscores_bf = dscores.astype(jnp.bfloat16)
    value_part = jnp.einsum("hqk,qhd->kd", probs_bf, grad_mine, preferred_element_type=jnp.float32)
    key_part = (
        jnp.einsum("hqk,qhd->kd", dscores_bf, query_mine, preferred_element_type=jnp.float32)
        * score_scale
    )
    query_part = (
        jnp.einsum("hqk,kd->qhd", dscores_bf, key_mine, preferred_element_type=jnp.float32)
        * score_scale
    )
    query_round = query_part.astype(jnp.bfloat16)
    query_send = jnp.dot(
        compact_back, query_round.reshape(spans, SPAN * width), preferred_element_type=jnp.float32
    )
    query_send = query_send.astype(jnp.bfloat16).reshape(owners, slot_count * SPAN, width)
    query_back = lax.all_to_all(query_send, "seq", split_axis=0, concat_axis=0, tiled=True)
    query_rows_out = jnp.dot(
        to_slot_bf,
        query_back.reshape(owners * slot_count, SPAN * width),
        preferred_element_type=jnp.float32,
    )
    query_out = query_rows_out.reshape(tok_dev, width).astype(jnp.bfloat16)

    def after_owner(running):
        nearby = passed_along(running, "head", -1)
        wrapped = passed_along(running, "head", GROUP // HQ_DEV - 1)
        return jnp.where(position == members - 1, wrapped, nearby)

    summed = group_total(jnp.stack([key_part.T, value_part.T]), members, position, after_owner)
    share = summed.shape[1]

    def send_share(part):
        rows = part.reshape(share, NLIST, KVCH).transpose(1, 2, 0).reshape(NLIST, KVCH * share)
        return jnp.dot(kv_compact.T, rows, precision=HIGH).reshape(owners, kv_count * KVCH, share)

    key_back, value_back = sent_together_2(
        (send_share(summed[0]), send_share(summed[1])), "seq", 0, 0, 1
    )

    def home_share(got):
        rows = jnp.dot(select.T, got.reshape(owners * kv_count, KVCH * share), precision=HIGH)
        return rows.reshape(tok_dev, share).T

    return (query_out, home_share(key_back), home_share(value_back))


def solution(mesh):
    placed = (
        P("seq", "head"),
        P("seq", None),
        P("seq", None),
        P("seq", "head"),
        P("head", "seq"),
        P("head", "seq"),
        P(),
        P(),
        P(),
    )
    return jax.shard_map(
        local,
        mesh=mesh,
        in_specs=placed,
        out_specs=(P("seq", "head"), P("head", "seq"), P("head", "seq")),
        check_vma=False,
    )
```

profile of v0, /device:TPU:1, one launch (start us, length us, event | category | flops | bytes accessed | tf_op | source)
XLA Modules:
  0.0 216.9 jit_solution(8981365124238008976)
XLA Ops:
  0.7 0.8 copy.161
  1.7 0.8 copy.164
  2.8 2.6 %convert_reduce_fusion = s32[64,64]{1,0:T(8,128)S(1)} fusion(s32[64,64]{1,0:T(8,128)} %param.15, pred[64,64]{1,0:T(8,128)(4,1)S(1)} %iota_compare_fusion.7), kind=kLoop, calls=%fused_computation.20 | loop fusion | flops 1044480 | bytes 36864 | tf_op jit(solution)/shard_map/reduce_sum | solution.py:48
  7.3 14.5 %all-to-all-start.1 = ((f32[64,16,4]{1,2,0:T(4,128)}), f32[64,16,4]{1,2,0:T(4,128)S(1)}, u32[]{:S(2)}, u32[]{:S(2)}) async-start(f32[64,16,4]{1,2,0:T(4,128)} %copy.167), calls=%async_computation.1 | async-start | bytes 262144 | tf_op jit(solution)/shard_map/all_to_all | solution.py:34
  23.6 1.0 constant_dynamic-slice_fusion.1
  26.0 1.1 convolution_convert_fusion.7
  27.6 1.2 maximum_bitcast_fusion
  29.3 2.9 %reduce.6 = bf16[64,16384]{1,0:T(8,128)(2,1)} reduce(bf16[64,1,16384]{2,0,1:T(8,128)(2,1)S(1)} %maximum_bitcast_fusion, bf16[]{:T(256)} %broadcast.142), dimensions={1}, to_apply=%copy.159.reduce_sub_computation | reduce | bytes 4194306 | tf_op jit(solution)/shard_map/all_to_all | solution.py:24
  32.2 4.5 %reshape.315 = bf16[64,2,8192]{2,1,0:T(2,128)(2,1)} reshape(bf16[64,16384]{1,0:T(8,128)(2,1)} %reduce.6) | data formatting | bytes 4194304
  36.7 10.6 %all-to-all-start = ((bf16[64,2,8192]{2,1,0:T(2,128)(2,1)}), bf16[64,2,8192]{2,1,0:T(2,128)(2,1)S(1)}, u32[]{:S(2)}, u32[]{:S(2)}) async-start(bf16[64,2,8192]{2,1,0:T(2,128)(2,1)} %reshape.315), calls=%async_computation | async-start | bytes 4194304 | tf_op jit(solution)/shard_map/all_to_all | solution.py:24
  51.9 45.0 %all-to-all-done = bf16[64,2,8192]{2,1,0:T(2,128)(2,1)S(1)} async-done(((bf16[64,2,8192]{2,1,0:T(2,128)(2,1)}), bf16[64,2,8192]{2,1,0:T(2,128)(2,1)S(1)}, u32[]{:S(2)}, u32[]{:S(2)}) %all-to-all-start) | async-done | bytes 2097184 | tf_op jit(solution)/shard_map/all_to_all | solution.py:24
  97.0 6.8 %reshape.316 = bf16[64,1,16384]{2,1,0:T(2,128)(2,1)} reshape(bf16[64,2,8192]{2,1,0:T(2,128)(2,1)S(1)} %all-to-all-done) | data formatting | bytes 4194304
  103.7 4.5 %copy.214 = bf16[64,1,16384]{2,0,1:T(8,128)(2,1)S(1)} copy(bf16[64,1,16384]{2,1,0:T(2,128)(2,1)} %reshape.316) | data formatting | bytes 4194304
  111.6 1.1 fusion.11
  112.7 2.6 %fusion.1 = bf16[4,512,512]{1,2,0:T(8,128)(2,1)S(1)} fusion(f32[512,512,4]{1,0,2:T(8,128)S(1)} %fusion.73, bf16[512,128,1]{1,0,2:T(8,128)(2,1)S(1)} %reshape.305, bf16[512,4,128]{0,2,1:T(8,128)(2,1)} %copy-done.2, f32[4,512]{1,0:T(4,128)S(1)} %copy.174, f32[4,512]{1,0:T(4,128)S(1)} %copy.170, pred[512,512]{0,1:T(8,128)(4,1)} %copy-done.4), kind=kOutput, calls=%fused_computation.12 | convolution fusion | flops 274726912 | bytes 7225344 | tf_op jit(solution)/shard_map/qhd,kd->hqk/dot_general | solution.py:196
  116.1 1.3 collective-permute-start.1
  117.4 5.2 %collective-permute-start = (f32[2,32,512]{2,1,0:T(8,128)S(1)}, f32[2,32,512]{2,1,0:T(8,128)S(1)}, u32[]{:S(2)}, u32[]{:S(2)}) collective-permute-start(f32[2,32,512]{2,1,0:T(8,128)S(1)} %fusion.33), channel_id=1, source_target_pairs={{0,3},{1,4},{2,5},{3,6},{4,7},{5,8},{6,9},{7,10},{8,11},{12,15},{1... | collective-permute-start | bytes 393224 | tf_op jit(solution)/shard_map/ppermute | solution.py:41
  122.8 1.8 collective-permute-done
  124.6 1.3 collective-permute-start.3
  125.9 16.2 %collective-permute-start.2 = (f32[2,32,512]{2,1,0:T(8,128)S(1)}, f32[2,32,512]{2,1,0:T(8,128)}, u32[]{:S(2)}, u32[]{:S(2)}) collective-permute-start(f32[2,32,512]{2,1,0:T(8,128)S(1)} %fusion.35), channel_id=1, source_target_pairs={{0,3},{1,4},{2,5},{3,6},{4,7},{5,8},{6,9},{7,10},{8,11},{12,15},{1... | collective-permute-start | bytes 393224 | tf_op jit(solution)/shard_map/ppermute | solution.py:41
  143.7 0.9 fusion.37
  144.6 1.3 collective-permute-start.5
  145.9 13.4 %collective-permute-start.4 = (f32[2,32,512]{2,1,0:T(8,128)S(1)}, f32[2,32,512]{2,1,0:T(8,128)S(1)}, u32[]{:S(2)}, u32[]{:S(2)}) collective-permute-start(f32[2,32,512]{2,1,0:T(8,128)S(1)} %fusion.37), channel_id=1, source_target_pairs={{0,3},{1,4},{2,5},{3,6},{4,7},{5,8},{6,9},{7,10},{8,11},{12,15},{1... | collective-permute-start | bytes 393224 | tf_op jit(solution)/shard_map/ppermute | solution.py:41
  159.6 1.0 copy.203
  160.6 7.5 %all-to-all-start.2 = ((bf16[64,8,512]{2,1,0:T(8,128)(2,1)}), bf16[64,8,512]{2,1,0:T(8,128)(2,1)S(1)}, u32[]{:S(2)}, u32[]{:S(2)}) async-start(bf16[64,8,512]{2,1,0:T(8,128)(2,1)} %bitcast.40), calls=%async_computation.2 | async-start | bytes 1048576 | tf_op jit(solution)/shard_map/all_to_all | solution.py:214
  170.5 1.1 copy.186
  171.6 1.4 reshape.317
  173.0 12.8 %all-to-all-done.2 = bf16[64,8,512]{2,1,0:T(8,128)(2,1)S(1)} async-done(((bf16[64,8,512]{2,1,0:T(8,128)(2,1)}), bf16[64,8,512]{2,1,0:T(8,128)(2,1)S(1)}, u32[]{:S(2)}, u32[]{:S(2)}) %all-to-all-start.2) | async-done | bytes 524320 | tf_op jit(solution)/shard_map/all_to_all | solution.py:214
  185.8 5.7 %all-to-all-start.3 = ((f32[64,1,2048]{2,1,0:T(1,128)}), f32[64,1,2048]{2,1,0:T(1,128)S(1)}, u32[]{:S(2)}, u32[]{:S(2)}) async-start(f32[64,1,2048]{2,1,0:T(1,128)} %reshape.317), calls=%async_computation.3 | async-start | bytes 1048576 | tf_op jit(solution)/shard_map/all_to_all | solution.py:34
  192.1 1.0 convert_element_type.117
  193.1 16.1 %all-to-all-done.3 = f32[64,1,2048]{2,1,0:T(1,128)S(1)} async-done(((f32[64,1,2048]{2,1,0:T(1,128)}), f32[64,1,2048]{2,1,0:T(1,128)S(1)}, u32[]{:S(2)}, u32[]{:S(2)}) %all-to-all-start.3) | async-done | bytes 524320 | tf_op jit(solution)/shard_map/all_to_all | solution.py:34
  209.7 1.9 reduce.7
  (120 shorter events, 25.4 us)
Async XLA Ops:
  2.6 23.2 %copy-start = (bf16[512,512]{1,0:T(8,128)(2,1)S(1)}, bf16[512,512]{1,0:T(8,128)(2,1)}, u32[]{:S(2)}) copy-start(bf16[512,512]{1,0:T(8,128)(2,1)} %param.9) | copy-start | bytes 1572868
  7.3 29.4 %all-to-all-start.1 = ((f32[64,16,4]{1,2,0:T(4,128)}), f32[64,16,4]{1,2,0:T(4,128)S(1)}, u32[]{:S(2)}, u32[]{:S(2)}) async-start(f32[64,16,4]{1,2,0:T(4,128)} %copy.167), calls=%async_computation.1 | async-start | bytes 262144 | tf_op jit(solution)/shard_map/all_to_all | solution.py:34
  24.7 2.4 %copy-start.1 = (bf16[512,512]{1,0:T(8,128)(2,1)S(1)}, bf16[512,512]{1,0:T(8,128)(2,1)}, u32[]{:S(2)}) copy-start(bf16[512,512]{1,0:T(8,128)(2,1)} %param.12) | copy-start | bytes 1572868
  36.7 10.6 %copy-start.5 = (s32[64,16]{0,1:T(8,128)S(1)}, s32[64,16]{0,1:T(8,128)}, u32[]{:S(2)}) copy-start(s32[64,16]{0,1:T(8,128)} %param.16) | copy-start | bytes 12292
  36.7 11.0 %copy-start.6 = (s32[64,64]{1,0:T(8,128)S(1)}, s32[64,64]{1,0:T(8,128)}, u32[]{:S(2)}) copy-start(s32[64,64]{1,0:T(8,128)} %param.17) | copy-start | bytes 49156
  36.7 11.2 %copy-start.3 = (s32[64,64]{1,0:T(8,128)S(1)}, s32[64,64]{1,0:T(8,128)}, u32[]{:S(2)}) copy-start(s32[64,64]{1,0:T(8,128)} %param.15) | copy-start | bytes 49156
  36.7 60.3 %all-to-all-start = ((bf16[64,2,8192]{2,1,0:T(2,128)(2,1)}), bf16[64,2,8192]{2,1,0:T(2,128)(2,1)S(1)}, u32[]{:S(2)}, u32[]{:S(2)}) async-start(bf16[64,2,8192]{2,1,0:T(2,128)(2,1)} %reshape.315), calls=%async_computation | async-start | bytes 4194304 | tf_op jit(solution)/shard_map/all_to_all | solution.py:24
  50.8 60.8 %copy-start.4 = (pred[512,512]{0,1:T(8,128)(4,1)}, pred[512,512]{0,1:T(8,128)(4,1)S(1)}, u32[]{:S(2)}) copy-start(pred[512,512]{0,1:T(8,128)(4,1)S(1)} %compare_and_fusion) | copy-start | bytes 786436
  110.8 0.8 copy-start.2
  116.1 6.7 %collective-permute-start.1 = (f32[2,32,512]{2,1,0:T(8,128)S(1)}, f32[2,32,512]{2,1,0:T(8,128)S(1)}, u32[]{:S(2)}, u32[]{:S(2)}) collective-permute-start(f32[2,32,512]{2,1,0:T(8,128)S(1)} %fusion.33), channel_id=1, source_target_pairs={{1,0},{2,1},{3,2},{4,3},{5,4},{6,5},{7,6},{8,7},{9,8},{10,9},{11,1... | collective-permute-start | bytes 393224 | tf_op jit(solution)/shard_map/ppermute | solution.py:41
  117.4 7.1 %collective-permute-start = (f32[2,32,512]{2,1,0:T(8,128)S(1)}, f32[2,32,512]{2,1,0:T(8,128)S(1)}, u32[]{:S(2)}, u32[]{:S(2)}) collective-permute-start(f32[2,32,512]{2,1,0:T(8,128)S(1)} %fusion.33), channel_id=1, source_target_pairs={{0,3},{1,4},{2,5},{3,6},{4,7},{5,8},{6,9},{7,10},{8,11},{12,15},{1... | collective-permute-start | bytes 393224 | tf_op jit(solution)/shard_map/ppermute | solution.py:41
  124.6 18.7 %collective-permute-start.3 = (f32[2,32,512]{2,1,0:T(8,128)S(1)}, f32[2,32,512]{2,1,0:T(8,128)}, u32[]{:S(2)}, u32[]{:S(2)}) collective-permute-start(f32[2,32,512]{2,1,0:T(8,128)S(1)} %fusion.35), channel_id=1, source_target_pairs={{1,0},{2,1},{3,2},{4,3},{5,4},{6,5},{7,6},{8,7},{9,8},{10,9},{11,1... | collective-permute-start | bytes 393224 | tf_op jit(solution)/shard_map/ppermute | solution.py:41
  125.9 17.8 %collective-permute-start.2 = (f32[2,32,512]{2,1,0:T(8,128)S(1)}, f32[2,32,512]{2,1,0:T(8,128)}, u32[]{:S(2)}, u32[]{:S(2)}) collective-permute-start(f32[2,32,512]{2,1,0:T(8,128)S(1)} %fusion.35), channel_id=1, source_target_pairs={{0,3},{1,4},{2,5},{3,6},{4,7},{5,8},{6,9},{7,10},{8,11},{12,15},{1... | collective-permute-start | bytes 393224 | tf_op jit(solution)/shard_map/ppermute | solution.py:41
  144.6 23.6 %collective-permute-start.5 = (f32[2,32,512]{2,1,0:T(8,128)S(1)}, f32[2,32,512]{2,1,0:T(8,128)S(1)}, u32[]{:S(2)}, u32[]{:S(2)}) collective-permute-start(f32[2,32,512]{2,1,0:T(8,128)S(1)} %fusion.37), channel_id=1, source_target_pairs={{1,0},{2,1},{3,2},{4,3},{5,4},{6,5},{7,6},{8,7},{9,8},{10,9},{11,1... | collective-permute-start | bytes 393224 | tf_op jit(solution)/shard_map/ppermute | solution.py:41
  145.9 22.3 %collective-permute-start.4 = (f32[2,32,512]{2,1,0:T(8,128)S(1)}, f32[2,32,512]{2,1,0:T(8,128)S(1)}, u32[]{:S(2)}, u32[]{:S(2)}) collective-permute-start(f32[2,32,512]{2,1,0:T(8,128)S(1)} %fusion.37), channel_id=1, source_target_pairs={{0,3},{1,4},{2,5},{3,6},{4,7},{5,8},{6,9},{7,10},{8,11},{12,15},{1... | collective-permute-start | bytes 393224 | tf_op jit(solution)/shard_map/ppermute | solution.py:41
  160.6 25.2 %all-to-all-start.2 = ((bf16[64,8,512]{2,1,0:T(8,128)(2,1)}), bf16[64,8,512]{2,1,0:T(8,128)(2,1)S(1)}, u32[]{:S(2)}, u32[]{:S(2)}) async-start(bf16[64,8,512]{2,1,0:T(8,128)(2,1)} %bitcast.40), calls=%async_computation.2 | async-start | bytes 1048576 | tf_op jit(solution)/shard_map/all_to_all | solution.py:214
  185.8 23.4 %all-to-all-start.3 = ((f32[64,1,2048]{2,1,0:T(1,128)}), f32[64,1,2048]{2,1,0:T(1,128)S(1)}, u32[]{:S(2)}, u32[]{:S(2)}) async-start(f32[64,1,2048]{2,1,0:T(1,128)} %reshape.317), calls=%async_computation.3 | async-start | bytes 1048576 | tf_op jit(solution)/shard_map/all_to_all | solution.py:34
where the time goes:
time: 218 us; the launch traced here: 217 us
  starting transfers between devices  77.1 us (35%)
  waiting for transfers between devices  76.1 us (35%)
  local copies, waits for them, and re-layouts  34.8 us (16%)
  other arithmetic  13.8 us (6%)
  matrix products  13.7 us (6%)
    all_to_all x1, waiting for transfers between devices, sent_together(): lax.all_to_all(both, axis, split_axis=split_dim, concat_axis=concat_dim,...  45 us
    ppermute x6, starting transfers between devices, passed_along(): return lax.ppermute(value, axis, pairs)  38.7 us
    unnamed x23, local copies, waits for them, and re-layouts  20.3 us
    all_to_all x2, starting transfers between devices, sent_together_2(): lax.all_to_all(both, axis, split_axis=split_dim, concat_axis=concat_dim,...  20.2 us
    all_to_all x2, waiting for transfers between devices, sent_together_2(): lax.all_to_all(both, axis, split_axis=split_dim, concat_axis=concat_dim,...  16.1 us
    all_to_all x1, waiting for transfers between devices, local(): lax.all_to_all(query_send, 'seq', split_axis=0, concat_axis=0, tiled=True)  12.8 us
    all_to_all x1, starting transfers between devices, sent_together(): lax.all_to_all(both, axis, split_axis=split_dim, concat_axis=concat_dim,...  10.6 us
    all_to_all x1, starting transfers between devices, local(): lax.all_to_all(query_send, 'seq', split_axis=0, concat_axis=0, tiled=True)  7.54 us
  transfers between devices with their start and end apart: 10, of which 5 were waited for; matrix products, arithmetic and copies ran while one was open for 13% of the time, Pallas kernels for 0%

commit v1 on v0

v1 whole, which is shorter than its diff:
```python
import math

import jax
import jax.numpy as jnp
from jax import lax
from jax.experimental import pallas as pl
from jax.experimental.pallas import tpu as pltpu
from jax.sharding import Mesh
from jax.sharding import PartitionSpec as P

HD = 128
GROUP = 16
SPAN = 8
KVCH = 32
NLIST = 16
SEQ = 64
MEM = 4
HEADS = 4
TOK = 512
QROWS = HEADS * SPAN
STAT = 2 * QROWS
KVROW = STAT + SPAN
IN_ROWS = KVROW + 16
OUT_ROWS = QROWS + 16
QUART = HD // MEM
SCALE = 1.0 / math.sqrt(HD)
LOG2E = math.log2(math.e)
BF = jnp.bfloat16
F32 = jnp.float32


def lane_select(member):
    depth = lax.broadcasted_iota(jnp.int32, (HD, HD), 0)
    lane = lax.broadcasted_iota(jnp.int32, (HD, HD), 1) % 64
    key_hot = (depth == QUART * member + lane) & (lane < QUART)
    value_hot = (depth == QUART * member + lane - QUART) & (lane >= QUART)
    return key_hot.astype(F32).astype(BF), value_hot.astype(F32).astype(BF)


def pack_kernel(dest, sub, place, q_ref, g_ref, k_ref, v_ref, norm_ref, delta_ref, out_ref, stat, rows, kv):
    key_hot, value_hot = lane_select(place[1])
    both = jnp.dot(k_ref[...], key_hot, preferred_element_type=F32) + jnp.dot(
        v_ref[...], value_hot, preferred_element_type=F32
    )
    both = both.reshape(NLIST, 2, 16, HD)
    lane = lax.broadcasted_iota(jnp.int32, (NLIST, 16, HD), 2)
    kv[...] = jnp.where(lane < 64, both[:, 0], both[:, 1]).astype(BF)
    stat[...] = jnp.zeros_like(stat)
    for index, ref in enumerate((norm_ref, delta_ref)):
        value = ref[...]
        top = value.astype(BF).astype(F32)
        stat[8 * index : 8 * index + 4, :] = top
        stat[8 * index + 4 : 8 * index + 8, :] = value - top
    rows[...] = stat[...].T.astype(BF).reshape(SEQ, SPAN, HD)

    for j in range(SEQ):
        slot = dest[j]
        for h in range(HEADS):
            at = pl.ds(SPAN * h, SPAN)
            out_ref[slot, at, :] = q_ref[j, :, HD * h : HD * h + HD]
            at = pl.ds(QROWS + SPAN * h, SPAN)
            out_ref[slot, at, :] = g_ref[j, :, HD * h : HD * h + HD]
        out_ref[slot, pl.ds(STAT, SPAN), :] = rows[j]
        out_ref[j, pl.ds(KVROW, 16), :] = kv[sub[j]]


def vmem():
    return pl.BlockSpec(memory_space=pltpu.VMEM)


def smem():
    return pl.BlockSpec(memory_space=pltpu.SMEM)


def pack(dest, sub, place, q, g, k, v, norm, delta):
    head_block = pl.BlockSpec((TOK, HD), lambda i, d, s, p: (0, p[0]))
    whole = lambda shape: pl.BlockSpec(shape, lambda i, d, s, p: (0,) * len(shape))
    return pl.pallas_call(
        pack_kernel,
        out_shape=jax.ShapeDtypeStruct((SEQ, IN_ROWS, HD), BF),
        grid_spec=pltpu.PrefetchScalarGridSpec(
            num_scalar_prefetch=3,
            grid=(1,),
            in_specs=[
                whole((SEQ, SPAN, HEADS * HD)),
                whole((SEQ, SPAN, HEADS * HD)),
                head_block,
                head_block,
                whole((HEADS, TOK)),
                whole((HEADS, TOK)),
            ],
            out_specs=whole((SEQ, IN_ROWS, HD)),
            scratch_shapes=[
                pltpu.VMEM((HD, TOK), F32),
                pltpu.VMEM((SEQ, SPAN, HD), BF),
                pltpu.VMEM((NLIST, 16, HD), BF),
            ],
        ),
        name="pack",
    )(dest, sub, place, q.reshape(SEQ, SPAN, -1), g.reshape(SEQ, SPAN, -1), k, v, norm, delta)


def select_kernel(homes, got_ref, out_ref):
    for i in range(NLIST):
        block = got_ref[homes[i], pl.ds(KVROW, 16), :]
        for m in range(MEM):
            out_ref[m, i] = block


def select(homes, got):
    return pl.pallas_call(
        select_kernel,
        out_shape=jax.ShapeDtypeStruct((MEM, NLIST, 16, HD), BF),
        in_specs=[smem(), vmem()],
        out_specs=vmem(),
        name="select",
    )(homes, got)


def attend_kernel(got_ref, kv_ref, bias_ref, dq_ref, dkv_ref, key, value, stat):
    for half in range(2):
        total = jnp.zeros((NLIST * 16, 2 * HD), F32)
        lane = lax.broadcasted_iota(jnp.int32, (HD, 2 * HD), 0)
        col = lax.broadcasted_iota(jnp.int32, (HD, 2 * HD), 1)
        kind = col // HD
        for m in range(MEM):
            source = 64 * half + QUART * kind + (col % HD) - QUART * m
            good = (lane == source) & ((col % HD) // QUART == m)
            hot = good.astype(F32).astype(BF)
            total += jnp.dot(kv_ref[m].reshape(NLIST * 16, HD), hot, preferred_element_type=F32)
        total = total.astype(BF).reshape(NLIST, 16, 2 * HD)
        key[:, 16 * half : 16 * half + 16, :] = total[:, :, :HD]
        value[:, 16 * half : 16 * half + 16, :] = total[:, :, HD:]
    keys = key[...].reshape(TOK, HD)
    values = value[...].reshape(TOK, HD)
    stat[...] = got_ref[:, STAT : STAT + SPAN, :].reshape(TOK, HD).astype(F32)
    key_sum = jnp.zeros((HD, TOK), F32)
    value_sum = jnp.zeros((HD, TOK), F32)
    for h in range(HEADS):
        q = got_ref[:, SPAN * h : SPAN * h + SPAN, :].reshape(TOK, HD)
        g = got_ref[:, QROWS + SPAN * h : QROWS + SPAN * h + SPAN, :].reshape(TOK, HD)
        norm = stat[:, h : h + 1] + stat[:, 4 + h : 5 + h]
        delta = stat[:, 8 + h : 9 + h] + stat[:, 12 + h : 13 + h]
        scores = lax.dot_general(q, keys, (((1,), (1,)), ((), ())), preferred_element_type=F32)
        probs = jnp.exp2(scores * (SCALE * LOG2E) - norm * LOG2E + bias_ref[...])
        dprobs = lax.dot_general(g, values, (((1,), (1,)), ((), ())), preferred_element_type=F32)
        dscores = (probs * (dprobs - delta)).astype(BF)
        value_sum += lax.dot_general(g, probs.astype(BF), (((0,), (0,)), ((), ())), preferred_element_type=F32)
        key_sum += lax.dot_general(q, dscores, (((0,), (0,)), ((), ())), preferred_element_type=F32)
        dq = jnp.dot(dscores, keys, preferred_element_type=F32) * SCALE
        dq_ref[:, SPAN * h : SPAN * h + SPAN, :] = dq.astype(BF).reshape(SEQ, SPAN, HD)
    key_sum = key_sum * SCALE
    for m in range(MEM):
        dkv_ref[m, 0:QUART, :] = key_sum[QUART * m : QUART * m + QUART].astype(BF)
        dkv_ref[m, QUART : 2 * QUART, :] = value_sum[QUART * m : QUART * m + QUART].astype(BF)


def attend(got, kv, bias):
    return pl.pallas_call(
        attend_kernel,
        out_shape=(
            jax.ShapeDtypeStruct((SEQ, QROWS, HD), BF),
            jax.ShapeDtypeStruct((MEM, 2 * QUART, TOK), BF),
        ),
        in_specs=[vmem(), vmem(), vmem()],
        out_specs=(vmem(), vmem()),
        scratch_shapes=[
            pltpu.VMEM((NLIST, KVCH, HD), BF),
            pltpu.VMEM((NLIST, KVCH, HD), BF),
            pltpu.VMEM((TOK, HD), F32),
        ],
        name="attend",
    )(got, kv, bias)


def spread_kernel(homes, part_ref, dq_ref, out_ref):
    out_ref[:, 0:QROWS, :] = dq_ref[...]
    total = (part_ref[0].astype(F32) + part_ref[1].astype(F32)) + (
        part_ref[2].astype(F32) + part_ref[3].astype(F32)
    )
    lane = lax.broadcasted_iota(jnp.int32, (16, HD), 1) // KVCH
    for i in range(NLIST):
        tile, place = divmod(i, 4)
        block = jnp.zeros((16, HD), F32)
        for b in range(4):
            piece = total[16 * b : 16 * b + 16, HD * tile : HD * tile + HD]
            shift = (KVCH * (b - place)) % HD
            if shift:
                piece = pltpu.roll(piece, shift, 1)
            block = jnp.where(lane == b, piece, block)
        out_ref[homes[i], pl.ds(QROWS, 16), :] = block.astype(BF)


def spread(homes, part, dq):
    return pl.pallas_call(
        spread_kernel,
        out_shape=jax.ShapeDtypeStruct((SEQ, OUT_ROWS, HD), BF),
        in_specs=[smem(), vmem(), vmem()],
        out_specs=vmem(),
        name="spread",
    )(homes, part, dq)


def settle_kernel(dest, sub, got_ref, dq_ref, dk_ref, dv_ref, acc):
    acc[...] = jnp.zeros_like(acc)
    for j in range(SEQ):
        slot = dest[j]
        for h in range(HEADS):
            dq_ref[j, :, HD * h : HD * h + HD] = got_ref[slot, pl.ds(SPAN * h, SPAN), :]

    def add(n, carry):
        spot = sub[n]

        @pl.when(spot >= 0)
        def _():
            acc[spot] += got_ref[n, pl.ds(QROWS, 16), :].astype(F32)

        return carry

    lax.fori_loop(0, SEQ, add, 0)
    lane = lax.broadcasted_iota(jnp.int32, (16, HD), 1) // KVCH
    for ref, first in ((dk_ref, 0), (dv_ref, 2)):
        for b in range(2):
            for tile in range(4):
                block = jnp.zeros((16, HD), F32)
                for place in range(4):
                    piece = acc[4 * tile + place]
                    shift = (KVCH * (place - first - b)) % HD
                    if shift:
                        piece = pltpu.roll(piece, shift, 1)
                    block = jnp.where(lane == place, piece, block)
                ref[16 * b : 16 * b + 16, HD * tile : HD * tile + HD] = block


def settle(dest, sub, got):
    return pl.pallas_call(
        settle_kernel,
        out_shape=(
            jax.ShapeDtypeStruct((SEQ, SPAN, HEADS * HD), BF),
            jax.ShapeDtypeStruct((QUART, TOK), F32),
            jax.ShapeDtypeStruct((QUART, TOK), F32),
        ),
        in_specs=[smem(), smem(), vmem()],
        out_specs=(vmem(), vmem(), vmem()),
        scratch_shapes=[pltpu.VMEM((NLIST, 16, HD), F32)],
        name="settle",
    )(dest, sub, got)


def exchanged(value, axis):
    return lax.all_to_all(value, axis, split_axis=0, concat_axis=0, tiled=True)


def local(query_rows, key_rows, value_rows, output_grad, log_norm, row_delta, dispatch, listed_spans, range_start):
    home = lax.axis_index("seq")
    kv_head = lax.axis_index("kvh")
    member = lax.axis_index("mem")
    place = jnp.stack([kv_head, member]).astype(jnp.int32)
    dest = lax.dynamic_index_in_dim(dispatch, home, 0, keepdims=False)
    at_home = listed_spans // NLIST == home
    sub = jnp.sum(jnp.where(at_home, listed_spans % NLIST + 1, 0), axis=1) - 1
    sent = pack(dest, jnp.maximum(sub, 0), place, query_rows, output_grad, key_rows, value_rows, log_norm, row_delta)
    got = exchanged(sent, "seq")

    my_list = lax.dynamic_index_in_dim(listed_spans, home, 0, keepdims=False)
    homes = my_list // NLIST
    here = dispatch == home
    spot = jnp.arange(SEQ, dtype=jnp.int32)
    span_ids = jnp.sum(jnp.where(here, spot[:, None] * SEQ + spot[None, :], 0), axis=1)
    starts = jnp.sum(jnp.where(here, range_start, 0), axis=1)
    query_pos = (span_ids[:, None] * SPAN + jnp.arange(SPAN, dtype=jnp.int32)[None, :]).reshape(-1)
    lowest = jnp.repeat(starts, SPAN)
    key_pos = (my_list[:, None] * KVCH + jnp.arange(KVCH, dtype=jnp.int32)[None, :]).reshape(-1)
    allowed = (key_pos[None, :] <= query_pos[:, None]) & (key_pos[None, :] >= lowest[:, None])
    bias = jnp.where(allowed, 0.0, -1e30).astype(F32)

    chosen = select(homes, got)
    kv = exchanged(chosen, "mem")
    dq, dkv = attend(got, kv, bias)
    part = exchanged(dkv, "mem")
    back = exchanged(spread(homes, part, dq), "seq")
    dq_out, dk_out, dv_out = settle(dest, sub, back)
    return dq_out.reshape(TOK, HEADS * HD), dk_out, dv_out


def solution(mesh):
    seq, head = mesh.axis_names
    split = Mesh(mesh.devices.reshape(SEQ, -1, MEM), (seq, "kvh", "mem"))
    both = ("kvh", "mem")
    placed = (
        P("seq", both),
        P("seq", None),
        P("seq", None),
        P("seq", both),
        P(both, "seq"),
        P(both, "seq"),
        P(),
        P(),
        P(),
    )
    return jax.shard_map(
        local,
        mesh=split,
        in_specs=placed,
        out_specs=(P("seq", both), P(both, "seq"), P(both, "seq")),
        check_vma=False,
    )
```

time: 218 us -> 128 us (0.59)
  starting transfers between devices: 77.1 us -> 18.6 us
  blocking collectives: 0 us -> 44.4 us
  waiting for transfers between devices: 76.1 us -> 39.6 us
  local copies, waits for them, and re-layouts: 34.8 us -> 3.65 us
  Pallas kernels: 0 us -> 16.2 us
  matrix products: 13.7 us -> 0 us
  other arithmetic: 13.8 us -> 3.93 us
    all_to_all x0 -> x2, blocking collectives: none -> 44.4 us  [exchanged(): return lax.all_to_all(value, axis, split_axis=0, concat_axis=0, tiled=True)]
    ppermute x6 -> x0, starting transfers between devices: 38.7 us -> none  [passed_along(): return lax.ppermute(value, axis, pairs)]
    all_to_all x4 -> x2, waiting for transfers between devices: 74 us -> 39.6 us  [exchanged(): return lax.all_to_all(value, axis, split_axis=0, concat_axis=0, tiled=True)]
    all_to_all x4 -> x2, starting transfers between devices: 38.3 us -> 18.6 us  [exchanged(): return lax.all_to_all(value, axis, split_axis=0, concat_axis=0, tiled=True)]
    unnamed x23 -> x10, local copies, waits for them, and re-layouts: 20.3 us -> 1.84 us
    pallas_call x0 -> x5, Pallas kernels: none -> 16.2 us  [the longest x1 5.47 us: attend(): pl.pallas_call(attend_kernel, out_shape=(jax.ShapeDtypeStruct((SEQ, QROWS...]
    dot_general x25 -> x0, matrix products: 13.7 us -> none  [the longest x1 2.6 us: local(): jnp.einsum('qhd,kd->hqk', grad_mine, value_mine, preferred_element_type=j...]
    all_to_all x3 -> x0, other arithmetic: 5.94 us -> none  [the longest x2 4.06 us: sent_together(): lax.all_to_all(both, axis, split_axis=split_dim, concat_axis=concat_dim,...]
  transfers between devices with their start and end apart: 10 -> 2, of which waited for: 5 -> 2; matrix products, arithmetic and copies ran while one was open for 13% -> 2% of each run, Pallas kernels for 0% -> 0%
where the time goes in v1:
time: 128 us; the launch traced here: 127 us
  blocking collectives  44.4 us (35%)
  waiting for transfers between devices  39.6 us (31%)
  starting transfers between devices  18.6 us (15%)
  Pallas kernels  16.2 us (13%)
  other arithmetic  3.93 us (3%)
  local copies, waits for them, and re-layouts  3.65 us (3%)
    all_to_all x2, blocking collectives, exchanged(): return lax.all_to_all(value, axis, split_axis=0, concat_axis=0, tiled=True)  44.4 us
    all_to_all x2, waiting for transfers between devices, exchanged(): return lax.all_to_all(value, axis, split_axis=0, concat_axis=0, tiled=True)  39.6 us
    all_to_all x2, starting transfers between devices, exchanged(): return lax.all_to_all(value, axis, split_axis=0, concat_axis=0, tiled=True)  18.6 us
    pallas_call x1, Pallas kernels, attend(): pl.pallas_call(attend_kernel, out_shape=(jax.ShapeDtypeStruct((SEQ, QROWS...  5.47 us
    pallas_call x1, Pallas kernels, pack(): pl.pallas_call(pack_kernel, out_shape=jax.ShapeDtypeStruct((SEQ, IN_ROWS,...  3.44 us
    pallas_call x1, Pallas kernels, settle(): pl.pallas_call(settle_kernel, out_shape=(jax.ShapeDtypeStruct((SEQ, SPAN,...  3.03 us
  transfers between devices with their start and end apart: 2, of which 2 were waited for; matrix products, arithmetic and copies ran while one was open for 2% of the time, Pallas kernels for 0%

profile of v1, /device:TPU:1, one launch (start us, length us, event | category | flops | bytes accessed | tf_op | source)
XLA Modules:
  0.0 127.1 jit_solution(2592923012198199141)
XLA Ops:
  0.6 0.7 fusion.3
  1.4 0.5 broadcast_maximum_fusion
  1.9 1.3 %dynamic-slice_bitcast_fusion.dest = s32[64]{0:T(128)} fusion(s32[64,64]{1,0:T(8,128)} %param.15, s32[]{:T(128)S(6)} %select_n.38), kind=kLoop, calls=%fused_computation.25 | loop fusion | bytes 516 | tf_op jit(solution)/shard_map/jit(dynamic_index_in_dim)/squeeze | solution.py:259
  3.2 0.6 pad_add_fusion.place
  3.8 3.4 %pack.1 = bf16[64,88,128]{2,1,0:T(8,128)(2,1)} custom-call(s32[64]{0:T(128)} %dynamic-slice_bitcast_fusion.dest, s32[64]{0:T(128)} %get-tuple-element.17.sub, s32[2]{0:T(128)} %pad_add_fusion.place, bf16[64,8,512]{2,1,0:T(8,128)(2,1)} %bitcast.7, bf16[64,8,512]{2,1,0:T(8,128)(2,1)} %bitcast.8, bf16[512,384]{1,0:T(8,128)(2,1)} %k_ref.1, ...), custom_call_target="tpu_custom_call" | custom-call | tf_op jit(solution)/shard_map/pack/pallas_call | solution.py:78
  7.3 0.0 copy-start.2
  7.3 0.0 copy-start.3
  7.3 14.7 %all-to-all-start = ((bf16[64,88,128]{2,1,0:T(8,128)(2,1)}), bf16[64,88,128]{2,1,0:T(8,128)(2,1)S(1)}, u32[]{:S(2)}, u32[]{:S(2)}) async-start(bf16[64,88,128]{2,1,0:T(8,128)(2,1)} %pack.1), calls=%async_computation | async-start | bytes 2883584 | tf_op jit(solution)/shard_map/all_to_all | solution.py:251
  22.0 0.0 copy-done.2
  22.0 0.2 dynamic-slice_reduce_fusion
  22.2 0.5 broadcast_multiply_fusion.1
  22.7 0.1 iota_add_fusion.1
  22.8 0.1 add.78
  22.9 0.0 copy-done.3
  22.9 0.0 copy-done.4
  22.9 0.2 select_reduce_fusion.1
  23.1 0.1 broadcast_in_dim.25
  23.1 0.1 ge.6
  23.2 35.2 %all-to-all-done.got_ref = bf16[64,88,128]{2,1,0:T(8,128)(2,1)S(1)} async-done(((bf16[64,88,128]{2,1,0:T(8,128)(2,1)}), bf16[64,88,128]{2,1,0:T(8,128)(2,1)S(1)}, u32[]{:S(2)}, u32[]{:S(2)}) %all-to-all-start) | async-done | bytes 1441824 | tf_op jit(solution)/shard_map/all_to_all | solution.py:251
  58.5 1.1 copy-done
  59.6 2.1 %select.11 = bf16[4,16,16,128]{3,2,1,0:T(8,128)(2,1)} custom-call(s32[16]{0:T(128)} %get-tuple-element.16.homes, bf16[64,88,128]{2,1,0:T(8,128)(2,1)} %copy-done), custom_call_target="tpu_custom_call" | custom-call | tf_op jit(solution)/shard_map/select/pallas_call | solution.py:111
  61.7 3.9 %all-to-all-start.1 = ((bf16[4,16,16,128]{3,2,1,0:T(8,128)(2,1)}), bf16[4,16,16,128]{3,2,1,0:T(8,128)(2,1)S(1)}, u32[]{:S(2)}, u32[]{:S(2)}) async-start(bf16[4,16,16,128]{3,2,1,0:T(8,128)(2,1)} %select.11), calls=%async_computation.1 | async-start | bytes 524288 | tf_op jit(solution)/shard_map/all_to_all | solution.py:251
  65.6 0.1 iota_add_fusion
  65.7 0.1 add.85
  65.8 1.2 and_select_fusion.bias_ref
  67.0 4.4 %all-to-all-done.1.kv_ref = bf16[4,16,16,128]{3,2,1,0:T(8,128)(2,1)S(1)} async-done(((bf16[4,16,16,128]{3,2,1,0:T(8,128)(2,1)}), bf16[4,16,16,128]{3,2,1,0:T(8,128)(2,1)S(1)}, u32[]{:S(2)}, u32[]{:S(2)}) %all-to-all-start.1) | async-done | bytes 262176 | tf_op jit(solution)/shard_map/all_to_all | solution.py:251
  71.4 0.7 copy-done.1
  72.1 5.5 %attend.1 = (bf16[64,32,128]{2,1,0:T(8,128)(2,1)}, bf16[4,64,512]{2,1,0:T(8,128)(2,1)}) custom-call(bf16[64,88,128]{2,1,0:T(8,128)(2,1)} %copy-done, bf16[4,16,16,128]{3,2,1,0:T(8,128)(2,1)} %copy-done.1, f32[512,512]{1,0:T(8,128)} %and_select_fusion.bias_ref), custom_call_target="tpu_custom_call" | custom-call | tf_op jit(solution)/shard_map/attend/pallas_call | solution.py:159
  77.5 11.2 %all_to_all.20.part_ref = bf16[4,64,512]{2,1,0:T(8,128)(2,1)} all-to-all(bf16[4,64,512]{2,1,0:T(8,128)(2,1)} %get-tuple-element.8), channel_id=1, replica_groups=mesh['seq'=64,'kvh'=3,'mem'=4] {'mem'}, dimensions={0} | all-to-all | bytes 524288 | tf_op jit(solution)/shard_map/all_to_all | solution.py:251
  88.7 2.2 %spread.1 = bf16[64,48,128]{2,1,0:T(8,128)(2,1)} custom-call(s32[16]{0:T(128)} %get-tuple-element.16.homes, bf16[4,64,512]{2,1,0:T(8,128)(2,1)} %all_to_all.20.part_ref, bf16[64,32,128]{2,1,0:T(8,128)(2,1)} %get-tuple-element.9.dq_ref), custom_call_target="tpu_custom_call" | custom-call | tf_op jit(solution)/shard_map/spread/pallas_call | solution.py:195
  90.9 33.2 %all_to_all.21.got_ref = bf16[64,48,128]{2,1,0:T(8,128)(2,1)} all-to-all(bf16[64,48,128]{2,1,0:T(8,128)(2,1)} %spread.1), channel_id=1, replica_groups=mesh['seq'=64,'kvh'=3,'mem'=4] {'seq'}, dimensions={0} | all-to-all | bytes 1572864 | tf_op jit(solution)/shard_map/all_to_all | solution.py:251
  124.1 3.0 %settle.1 = (bf16[64,8,512]{2,1,0:T(8,128)(2,1)}, f32[32,512]{1,0:T(8,128)}, f32[32,512]{1,0:T(8,128)}) custom-call(s32[64]{0:T(128)} %dynamic-slice_bitcast_fusion.dest, s32[64]{0:T(128)} %get-tuple-element.18.sub, bf16[64,48,128]{2,1,0:T(8,128)(2,1)} %all_to_all.21.got_ref), custom_call_target="tpu_custom_call" | custom-call | tf_op jit(solution)/shard_map/settle/pallas_call | solution.py:236
  (5 shorter events, 0.0 us)
Async XLA Ops:
  7.3 14.7 %copy-start.2 = (s32[64,16]{0,1:T(8,128)S(1)}, s32[64,16]{0,1:T(8,128)}, u32[]{:S(2)}) copy-start(s32[64,16]{0,1:T(8,128)} %param.16) | copy-start | bytes 12292
  7.3 15.6 %copy-start.3 = (s32[64,64]{1,0:T(8,128)S(1)}, s32[64,64]{1,0:T(8,128)}, u32[]{:S(2)}) copy-start(s32[64,64]{1,0:T(8,128)} %param.15) | copy-start | bytes 49156
  7.3 15.6 %copy-start.4 = (s32[64,64]{1,0:T(8,128)S(1)}, s32[64,64]{1,0:T(8,128)}, u32[]{:S(2)}) copy-start(s32[64,64]{1,0:T(8,128)} %param.17) | copy-start | bytes 49156
  7.3 51.2 %all-to-all-start = ((bf16[64,88,128]{2,1,0:T(8,128)(2,1)}), bf16[64,88,128]{2,1,0:T(8,128)(2,1)S(1)}, u32[]{:S(2)}, u32[]{:S(2)}) async-start(bf16[64,88,128]{2,1,0:T(8,128)(2,1)} %pack.1), calls=%async_computation | async-start | bytes 2883584 | tf_op jit(solution)/shard_map/all_to_all | solution.py:251
  58.5 1.1 copy-start
  61.7 9.7 %all-to-all-start.1 = ((bf16[4,16,16,128]{3,2,1,0:T(8,128)(2,1)}), bf16[4,16,16,128]{3,2,1,0:T(8,128)(2,1)S(1)}, u32[]{:S(2)}, u32[]{:S(2)}) async-start(bf16[4,16,16,128]{3,2,1,0:T(8,128)(2,1)} %select.11), calls=%async_computation.1 | async-start | bytes 524288 | tf_op jit(solution)/shard_map/all_to_all | solution.py:251
  71.4 0.7 copy-start.1

commit v2 on v1

v2 whole, which is shorter than its diff:
```python
import math

import jax
import jax.numpy as jnp
from jax import lax
from jax.experimental import pallas as pl
from jax.experimental.pallas import tpu as pltpu
from jax.sharding import Mesh
from jax.sharding import PartitionSpec as P

HD = 128
GROUP = 16
SPAN = 8
KVCH = 32
NLIST = 16
SEQ = 64
MEM = 4
HEADS = 4
TOK = 512
QROWS = HEADS * SPAN
HALF = HEADS // 2
HROWS = HALF * SPAN
ROWS_1 = 2 * HROWS + SPAN + 16
OUT_ROWS = QROWS + 16
QUART = HD // MEM
SCALE = 1.0 / math.sqrt(HD)
LOG2E = math.log2(math.e)
BF = jnp.bfloat16
PARAMS = pltpu.CompilerParams(vmem_limit_bytes=16 * 2**20)
F32 = jnp.float32


def lane_select(member):
    depth = lax.broadcasted_iota(jnp.int32, (HD, HD), 0)
    lane = lax.broadcasted_iota(jnp.int32, (HD, HD), 1) % 64
    key_hot = (depth == QUART * member + lane) & (lane < QUART)
    value_hot = (depth == QUART * member + lane - QUART) & (lane >= QUART)
    return key_hot.astype(F32).astype(BF), value_hot.astype(F32).astype(BF)


def first_kernel(
    dispatch_hbm, listed_hbm, norm_hbm, delta_hbm, q_hbm, g_hbm, k_hbm, v_hbm, out_ref,
    dispatch_ref, listed_ref, norm_ref, delta_ref, q_ref, g_ref, k_ref, v_ref,
    meta, where, stat, rows, kv, sems,
):
    home = lax.axis_index("seq")
    lanes = pl.ds(pl.multiple_of(lax.axis_index("kvh") * HD, HD), HD)
    half = pl.ds(0, HALF * HD)
    copies = [
        pltpu.make_async_copy(source, target, sems.at[index])
        for index, (source, target) in enumerate(
            (
                (dispatch_hbm, dispatch_ref),
                (listed_hbm, listed_ref),
                (norm_hbm, norm_ref),
                (delta_hbm, delta_ref),
                (k_hbm.at[:, lanes], k_ref),
                (v_hbm.at[:, lanes], v_ref),
                (q_hbm.at[:, :, half], q_ref),
                (g_hbm.at[:, :, half], g_ref),
            )
        )
    ]
    for copy in copies:
        copy.start()
    copies[0].wait()
    copies[1].wait()
    row = lax.broadcasted_iota(jnp.int32, (SEQ, SEQ), 0)
    listed = listed_ref[...]
    meta[0:1, 0:SEQ] = jnp.sum(jnp.where(row == home, dispatch_ref[...], 0), axis=0, keepdims=True)
    meta[1:2, 0:SEQ] = jnp.sum(jnp.where(listed // NLIST == home, listed % NLIST, 0), axis=0, keepdims=True)
    move = pltpu.make_async_copy(meta, where, sems.at[8])
    move.start()
    copies[2].wait()
    copies[3].wait()
    stat[...] = jnp.zeros_like(stat)
    for index, ref in enumerate((norm_ref, delta_ref)):
        value = ref[...]
        top = value.astype(BF).astype(F32)
        stat[8 * index : 8 * index + 4, :] = top
        stat[8 * index + 4 : 8 * index + 8, :] = value - top
    rows[...] = stat[...].T.astype(BF).reshape(SEQ, SPAN, HD)
    key_hot, value_hot = lane_select(lax.axis_index("mem"))
    copies[4].wait()
    copies[5].wait()
    both = jnp.dot(k_ref[...], key_hot, preferred_element_type=F32) + jnp.dot(
        v_ref[...], value_hot, preferred_element_type=F32
    )
    both = both.reshape(NLIST, 2, 16, HD)
    lane = lax.broadcasted_iota(jnp.int32, (NLIST, 16, HD), 2)
    kv[...] = jnp.where(lane < 64, both[:, 0], both[:, 1]).astype(BF)
    copies[6].wait()
    copies[7].wait()
    move.wait()
    for j in range(SEQ):
        slot = where[0, j]
        for h in range(HALF):
            out_ref[slot, pl.ds(SPAN * h, SPAN), :] = q_ref[j, :, HD * h : HD * h + HD]
            out_ref[slot, pl.ds(HROWS + SPAN * h, SPAN), :] = g_ref[j, :, HD * h : HD * h + HD]
        out_ref[slot, pl.ds(2 * HROWS, SPAN), :] = rows[j]
        out_ref[j, pl.ds(2 * HROWS + SPAN, 16), :] = kv[where[1, j]]


def vmem():
    return pl.BlockSpec(memory_space=pltpu.VMEM)


def smem():
    return pl.BlockSpec(memory_space=pltpu.SMEM)


def far():
    return pl.BlockSpec(memory_space=pltpu.HBM)


def first(dispatch, listed, norm, delta, q, g, k, v):
    return pl.pallas_call(
        first_kernel,
        out_shape=jax.ShapeDtypeStruct((SEQ, ROWS_1, HD), BF),
        in_specs=[far()] * 8,
        out_specs=vmem(),
        scratch_shapes=[
            pltpu.VMEM((SEQ, SEQ), jnp.int32),
            pltpu.VMEM((NLIST, SEQ), jnp.int32),
            pltpu.VMEM((HEADS, TOK), F32),
            pltpu.VMEM((HEADS, TOK), F32),
            pltpu.VMEM((SEQ, SPAN, HALF * HD), BF),
            pltpu.VMEM((SEQ, SPAN, HALF * HD), BF),
            pltpu.VMEM((TOK, HD), BF),
            pltpu.VMEM((TOK, HD), BF),
            pltpu.VMEM((8, HD), jnp.int32),
            pltpu.SMEM((8, HD), jnp.int32),
            pltpu.VMEM((HD, TOK), F32),
            pltpu.VMEM((SEQ, SPAN, HD), BF),
            pltpu.VMEM((NLIST, 16, HD), BF),
            pltpu.SemaphoreType.DMA((9,)),
        ],
        name="first",
    )(dispatch, listed.T, norm, delta, q, g, k, v)


def second_kernel(dest, q_ref, g_ref, out_ref):
    for j in range(SEQ):
        slot = dest[j]
        for h in range(HALF):
            out_ref[slot, pl.ds(SPAN * h, SPAN), :] = q_ref[j, :, HD * h : HD * h + HD]
            out_ref[slot, pl.ds(HROWS + SPAN * h, SPAN), :] = g_ref[j, :, HD * h : HD * h + HD]


def second(dest, q, g):
    half = pl.BlockSpec((SEQ, SPAN, HALF * HD), lambda i, d: (0, 0, 1))
    return pl.pallas_call(
        second_kernel,
        out_shape=jax.ShapeDtypeStruct((SEQ, 2 * HROWS, HD), BF),
        grid_spec=pltpu.PrefetchScalarGridSpec(
            num_scalar_prefetch=1,
            grid=(1,),
            in_specs=[half, half],
            out_specs=pl.BlockSpec((SEQ, 2 * HROWS, HD), lambda i, d: (0, 0, 0)),
        ),
        compiler_params=PARAMS,
        name="second",
    )(dest, q, g)


def select_kernel(homes, got_ref, out_ref):
    for i in range(NLIST):
        out_ref[i] = got_ref[homes[i], pl.ds(2 * HROWS + SPAN, 16), :]


def select(homes, got):
    return pl.pallas_call(
        select_kernel,
        out_shape=pltpu.VMEM((NLIST, 16, HD), BF),
        in_specs=[smem(), vmem()],
        out_specs=vmem(),
        compiler_params=PARAMS,
        name="select",
    )(homes, got)


def heads(q_at, g_at, stat, keys, values, bias_ref, dq_ref, base, key_sum, value_sum):
    for h in range(HALF):
        q = q_at(h)
        g = g_at(h)
        i = base + h
        norm = stat[:, i : i + 1] + stat[:, 4 + i : 5 + i]
        delta = stat[:, 8 + i : 9 + i] + stat[:, 12 + i : 13 + i]
        scores = lax.dot_general(q, keys, (((1,), (1,)), ((), ())), preferred_element_type=F32)
        probs = jnp.exp2(scores * (SCALE * LOG2E) - norm * LOG2E + bias_ref[...])
        dprobs = lax.dot_general(g, values, (((1,), (1,)), ((), ())), preferred_element_type=F32)
        dscores = (probs * (dprobs - delta)).astype(BF)
        value_sum += lax.dot_general(g, probs.astype(BF), (((0,), (0,)), ((), ())), preferred_element_type=F32)
        key_sum += lax.dot_general(q, dscores, (((0,), (0,)), ((), ())), preferred_element_type=F32)
        dq = jnp.dot(dscores, keys, preferred_element_type=F32) * SCALE
        dq_ref[:, SPAN * h : SPAN * h + SPAN, :] = dq.astype(BF).reshape(SEQ, SPAN, HD)
    return key_sum, value_sum


def taker(ref, offset):
    return lambda h: ref[:, offset + SPAN * h : offset + SPAN * h + SPAN, :].reshape(TOK, HD)


def early_kernel(
    got_ref, kv0, kv1, kv2, kv3, bias_ref, dq_ref, sums_ref, both_ref, stat_ref, key, value,
):
    member = lax.axis_index("mem")
    lane = lax.broadcasted_iota(jnp.int32, (HD, 2 * HD), 0)
    col = lax.broadcasted_iota(jnp.int32, (HD, 2 * HD), 1)
    for half in range(2):
        total = jnp.zeros((NLIST * 16, 2 * HD), F32)
        for s, ref in enumerate((kv0, kv1, kv2, kv3)):
            owner = lax.rem(member + (MEM - s), MEM)
            source = 64 * half + QUART * (col // HD) + (col % HD) - QUART * owner
            good = (lane == source) & ((col % HD) // QUART == owner)
            hot = good.astype(F32).astype(BF)
            total += jnp.dot(ref[...].reshape(NLIST * 16, HD), hot, preferred_element_type=F32)
        total = total.astype(BF).reshape(NLIST, 16, 2 * HD)
        key[:, 16 * half : 16 * half + 16, :] = total[:, :, :HD]
        value[:, 16 * half : 16 * half + 16, :] = total[:, :, HD:]
    keys = key[...].reshape(TOK, HD)
    values = value[...].reshape(TOK, HD)
    both_ref[0] = keys
    both_ref[1] = values
    stat = got_ref[:, 2 * HROWS : 2 * HROWS + SPAN, :].reshape(TOK, HD).astype(F32)
    stat_ref[...] = stat
    zero = jnp.zeros((HD, TOK), F32)
    key_sum, value_sum = heads(
        taker(got_ref, 0), taker(got_ref, HROWS), stat_ref, keys, values, bias_ref, dq_ref, 0, zero, zero
    )
    sums_ref[0] = key_sum
    sums_ref[1] = value_sum


def early(got, kvs, bias):
    return pl.pallas_call(
        early_kernel,
        out_shape=(
            pltpu.VMEM((SEQ, HROWS, HD), BF),
            pltpu.VMEM((2, HD, TOK), F32),
            pltpu.VMEM((2, TOK, HD), BF),
            pltpu.VMEM((TOK, HD), F32),
        ),
        in_specs=[vmem()] * 6,
        out_specs=(vmem(),) * 4,
        scratch_shapes=[pltpu.VMEM((NLIST, KVCH, HD), BF), pltpu.VMEM((NLIST, KVCH, HD), BF)],
        compiler_params=PARAMS,
        name="early",
    )(got, *kvs, bias)


def late_kernel(got_ref, sums_ref, both_ref, stat_ref, bias_ref, dq_ref, dkv_ref):
    key_sum, value_sum = heads(
        taker(got_ref, 0), taker(got_ref, HROWS), stat_ref, both_ref[0], both_ref[1], bias_ref, dq_ref, HALF,
        sums_ref[0], sums_ref[1],
    )
    key_sum = key_sum * SCALE
    for m in range(MEM):
        dkv_ref[m, 0:QUART, :] = key_sum[QUART * m : QUART * m + QUART].astype(BF)
        dkv_ref[m, QUART : 2 * QUART, :] = value_sum[QUART * m : QUART * m + QUART].astype(BF)


def late(got, sums, both, stat, bias):
    return pl.pallas_call(
        late_kernel,
        out_shape=(
            pltpu.VMEM((SEQ, HROWS, HD), BF),
            jax.ShapeDtypeStruct((MEM, 2 * QUART, TOK), BF),
        ),
        in_specs=[vmem()] * 5,
        out_specs=(vmem(), vmem()),
        compiler_params=PARAMS,
        name="late",
    )(got, sums, both, stat, bias)


def spread_kernel(homes, part_ref, early_ref, late_ref, out_ref):
    out_ref[:, 0:HROWS, :] = early_ref[...]
    out_ref[:, HROWS:QROWS, :] = late_ref[...]
    total = (part_ref[0].astype(F32) + part_ref[1].astype(F32)) + (
        part_ref[2].astype(F32) + part_ref[3].astype(F32)
    )
    lane = lax.broadcasted_iota(jnp.int32, (16, HD), 1) // KVCH
    for i in range(NLIST):
        tile, place = divmod(i, 4)
        block = jnp.zeros((16, HD), F32)
        for b in range(4):
            piece = total[16 * b : 16 * b + 16, HD * tile : HD * tile + HD]
            shift = (KVCH * (b - place)) % HD
            if shift:
                piece = pltpu.roll(piece, shift, 1)
            block = jnp.where(lane == b, piece, block)
        out_ref[homes[i], pl.ds(QROWS, 16), :] = block.astype(BF)


def spread(homes, part, dq_early, dq_late):
    return pl.pallas_call(
        spread_kernel,
        out_shape=jax.ShapeDtypeStruct((SEQ, OUT_ROWS, HD), BF),
        in_specs=[smem(), vmem(), vmem(), vmem()],
        out_specs=vmem(),
        compiler_params=PARAMS,
        name="spread",
    )(homes, part, dq_early, dq_late)


def settle_kernel(dest, sub, got_ref, dq_ref, dk_ref, dv_ref, acc):
    acc[...] = jnp.zeros_like(acc)
    for j in range(SEQ):
        slot = dest[j]
        for h in range(HEADS):
            dq_ref[j, :, HD * h : HD * h + HD] = got_ref[slot, pl.ds(SPAN * h, SPAN), :]

    for n in range(SEQ):
        acc[sub[n]] += got_ref[n, pl.ds(QROWS, 16), :].astype(F32)
    lane = lax.broadcasted_iota(jnp.int32, (16, HD), 1) // KVCH
    for ref, first in ((dk_ref, 0), (dv_ref, 2)):
        for b in range(2):
            for tile in range(4):
                block = jnp.zeros((16, HD), F32)
                for place in range(4):
                    piece = acc[4 * tile + place]
                    shift = (KVCH * (place - first - b)) % HD
                    if shift:
                        piece = pltpu.roll(piece, shift, 1)
                    block = jnp.where(lane == place, piece, block)
                ref[16 * b : 16 * b + 16, HD * tile : HD * tile + HD] = block


def settle(dest, sub, got):
    return pl.pallas_call(
        settle_kernel,
        out_shape=(
            jax.ShapeDtypeStruct((SEQ, SPAN, HEADS * HD), BF),
            jax.ShapeDtypeStruct((QUART, TOK), F32),
            jax.ShapeDtypeStruct((QUART, TOK), F32),
        ),
        in_specs=[smem(), smem(), vmem()],
        out_specs=(vmem(), vmem(), vmem()),
        scratch_shapes=[pltpu.VMEM((NLIST + 1, 16, HD), F32)],
        compiler_params=PARAMS,
        name="settle",
    )(dest, sub, got)


def near(value):
    return pltpu.with_memory_space_constraint(value, pltpu.VMEM)


def exchanged(value, axis):
    return near(lax.all_to_all(value, axis, split_axis=0, concat_axis=0, tiled=True))


def local(query_rows, key_rows, value_rows, output_grad, log_norm, row_delta, dispatch, listed_spans, range_start):
    home = lax.axis_index("seq")
    q = query_rows.reshape(SEQ, SPAN, HEADS * HD)
    g = output_grad.reshape(SEQ, SPAN, HEADS * HD)
    got_1 = exchanged(
        first(dispatch, listed_spans, log_norm, row_delta, q, g, key_rows, value_rows), "seq"
    )

    dest = lax.dynamic_index_in_dim(dispatch, home, 0, keepdims=False)
    at_home = listed_spans // NLIST == home
    sub = jnp.sum(jnp.where(at_home, listed_spans % NLIST - NLIST, 0), axis=1) + NLIST
    got_2 = exchanged(second(dest, q, g), "seq")
    my_list = lax.dynamic_index_in_dim(listed_spans, home, 0, keepdims=False)
    homes = my_list // NLIST
    here = dispatch == home
    spot = jnp.arange(SEQ, dtype=jnp.int32)
    span_ids = jnp.sum(jnp.where(here, spot[:, None] * SEQ + spot[None, :], 0), axis=1)
    starts = jnp.sum(jnp.where(here, range_start, 0), axis=1)
    query_pos = (span_ids[:, None] * SPAN + jnp.arange(SPAN, dtype=jnp.int32)[None, :]).reshape(-1)
    lowest = jnp.repeat(starts, SPAN)
    key_pos = (my_list[:, None] * KVCH + jnp.arange(KVCH, dtype=jnp.int32)[None, :]).reshape(-1)
    allowed = (key_pos[None, :] <= query_pos[:, None]) & (key_pos[None, :] >= lowest[:, None])
    bias = jnp.where(allowed, 0.0, -1e30).astype(F32)

    chosen = near(select(homes, got_1))
    kvs = [chosen] + [
        near(lax.ppermute(chosen, "mem", [(i, (i + s) % MEM) for i in range(MEM)])) for s in range(1, MEM)
    ]
    bias = near(bias)
    dq_early, sums, both, stat = map(near, early(got_1, kvs, bias))
    dq_late, dkv = late(got_2, sums, both, stat, bias)
    part = exchanged(dkv, "mem")
    back = exchanged(spread(homes, part, dq_early, near(dq_late)), "seq")
    dq_out, dk_out, dv_out = settle(dest, sub, back)
    return dq_out.reshape(TOK, HEADS * HD), dk_out, dv_out


def solution(mesh):
    seq, head = mesh.axis_names
    split = Mesh(mesh.devices.reshape(SEQ, -1, MEM), (seq, "kvh", "mem"))
    both = ("kvh", "mem")
    placed = (
        P("seq", both),
        P("seq", None),
        P("seq", None),
        P("seq", both),
        P(both, "seq"),
        P(both, "seq"),
        P(),
        P(),
        P(),
    )
    return jax.shard_map(
        local,
        mesh=split,
        in_specs=placed,
        out_specs=(P("seq", both), P(both, "seq"), P(both, "seq")),
        check_vma=False,
    )
```

time: 128 us -> 117 us (0.914)
  blocking collectives: 44.4 us -> 10.9 us
  starting transfers between devices: 18.6 us -> 40.5 us
  waiting for transfers between devices: 39.6 us -> 51.5 us
  Pallas kernels: 16.2 us -> 11.3 us
  other arithmetic: 3.93 us -> 0.58 us
  local copies, waits for them, and re-layouts: 3.65 us -> 1.26 us
    all_to_all x2 -> x1, blocking collectives: 44.4 us -> 10.9 us  [exchanged(): lax.all_to_all(value, axis, split_axis=0, concat_axis=0, tiled=True)]
    all_to_all x2 -> x3, starting transfers between devices: 18.6 us -> 31.5 us  [exchanged(): lax.all_to_all(value, axis, split_axis=0, concat_axis=0, tiled=True)]
    all_to_all x2 -> x3, waiting for transfers between devices: 39.6 us -> 48.6 us  [exchanged(): lax.all_to_all(value, axis, split_axis=0, concat_axis=0, tiled=True)]
    ppermute x0 -> x3, starting transfers between devices: none -> 9 us  [local(): lax.ppermute(chosen, 'mem', [(i, (i + s) % MEM) for i in range(MEM)])]
    pallas_call x3 -> x5, Pallas kernels: 11 us -> 7.91 us  [the longest x1 2.51 us: first(): pl.pallas_call(first_kernel, out_shape=jax.ShapeDtypeStruct((SEQ, ROWS_1,...]
    ppermute x0 -> x3, waiting for transfers between devices: none -> 2.82 us  [local(): lax.ppermute(chosen, 'mem', [(i, (i + s) % MEM) for i in range(MEM)])]
  transfers between devices with their start and end apart: 2 -> 6, of which waited for: 2 -> 5; matrix products, arithmetic and copies ran while one was open for 2% -> 1% of each run, Pallas kernels for 0% -> 3%
where the time goes in v2:
time: 117 us
  waiting for transfers between devices  51.5 us (44%)
  starting transfers between devices  40.5 us (35%)
  Pallas kernels  11.3 us (10%)
  blocking collectives  10.9 us (9%)
  local copies, waits for them, and re-layouts  1.26 us (1%)
    all_to_all x3, waiting for transfers between devices, exchanged(): lax.all_to_all(value, axis, split_axis=0, concat_axis=0, tiled=True)  48.6 us
    all_to_all x3, starting transfers between devices, exchanged(): lax.all_to_all(value, axis, split_axis=0, concat_axis=0, tiled=True)  31.5 us
    all_to_all x1, blocking collectives, exchanged(): lax.all_to_all(value, axis, split_axis=0, concat_axis=0, tiled=True)  10.9 us
    ppermute x3, starting transfers between devices, local(): lax.ppermute(chosen, 'mem', [(i, (i + s) % MEM) for i in range(MEM)])  9 us
    ppermute x3, waiting for transfers between devices, local(): lax.ppermute(chosen, 'mem', [(i, (i + s) % MEM) for i in range(MEM)])  2.82 us
    pallas_call x1, Pallas kernels, first(): pl.pallas_call(first_kernel, out_shape=jax.ShapeDtypeStruct((SEQ, ROWS_1,...  2.51 us
  transfers between devices with their start and end apart: 6, of which 5 were waited for; matrix products, arithmetic and copies ran while one was open for 1% of the time, Pallas kernels for 3%

profile of v2, /device:TPU:1, one launch (start us, length us, event | category | flops | bytes accessed | tf_op | source)
XLA Modules:
  0.0 116.8 jit_solution(9973045123981648569)
XLA Ops:
  0.6 2.5 %first.1 = bf16[64,56,128]{2,1,0:T(8,128)(2,1)} custom-call(s32[64,64]{1,0:T(8,128)} %dispatch_hbm.1, s32[16,64]{1,0:T(8,128)} %bitcast.10, f32[4,512]{1,0:T(4,128)} %norm_hbm.1, f32[4,512]{1,0:T(4,128)} %delta_hbm.1, bf16[64,8,512]{2,1,0:T(8,128)(2,1)} %bitcast.6, bf16[64,8,512]{2,1,0:T(8,128)(2,1)} %bitcast.8, bf16[512,384]{1,0:T(8,128)(2,1)} %k_hbm.1, ...), custom_call_target="tpu_custom_call" | custom-call | tf_op jit(solution)/shard_map/first/pallas_call | solution.py:117
  3.1 0.0 copy-start.4
  3.2 0.0 copy-start
  3.2 0.0 copy-start.1
  3.2 14.7 %all-to-all-start.1 = ((bf16[64,56,128]{2,1,0:T(8,128)(2,1)}), bf16[64,56,128]{2,1,0:T(8,128)(2,1)S(1)}, u32[]{:S(2)}, u32[]{:S(2)}) async-start(bf16[64,56,128]{2,1,0:T(8,128)(2,1)} %first.1), calls=%async_computation.1 | async-start | bytes 1835008 | tf_op jit(solution)/shard_map/all_to_all | solution.py:351
  18.0 1.4 %second.1 = bf16[64,32,128]{2,1,0:T(8,128)(2,1)} custom-call(s32[64]{0:T(128)S(1)} %dynamic-slice_bitcast_fusion.dest, bf16[64,8,512]{2,1,0:T(8,128)(2,1)S(1)} %bitcast.7, bf16[64,8,512]{2,1,0:T(8,128)(2,1)S(1)} %bitcast.9), custom_call_target="tpu_custom_call" | custom-call | tf_op jit(solution)/shard_map/second/pallas_call | solution.py:152
  19.4 0.2 dynamic-slice_reduce_fusion
  19.6 23.9 %all-to-all-done.1.got_ref = bf16[64,56,128]{2,1,0:T(8,128)(2,1)S(1)} async-done(((bf16[64,56,128]{2,1,0:T(8,128)(2,1)}), bf16[64,56,128]{2,1,0:T(8,128)(2,1)S(1)}, u32[]{:S(2)}, u32[]{:S(2)}) %all-to-all-start.1) | async-done | bytes 917536 | tf_op jit(solution)/shard_map/all_to_all | solution.py:351
  43.5 6.3 %all-to-all-start = ((bf16[64,32,128]{2,1,0:T(8,128)(2,1)}), bf16[64,32,128]{2,1,0:T(8,128)(2,1)S(1)}, u32[]{:S(2)}, u32[]{:S(2)}) async-start(bf16[64,32,128]{2,1,0:T(8,128)(2,1)} %second.1), calls=%async_computation | async-start | bytes 1048576 | tf_op jit(solution)/shard_map/all_to_all | solution.py:351
  49.8 0.1 iota_add_fusion.1
  49.9 0.1 add.81
  50.0 0.2 select_reduce_fusion.1
  50.2 0.1 iota_add_fusion
  50.2 0.1 add.88
  50.3 0.1 broadcast_in_dim.25
  50.4 0.1 ge.6
  50.5 0.6 select.11.kv0
  51.1 1.9 %collective-permute-start = (bf16[16,16,128]{2,1,0:T(8,128)(2,1)S(1)}, bf16[16,16,128]{2,1,0:T(8,128)(2,1)S(1)}, u32[]{:S(2)}, u32[]{:S(2)}) collective-permute-start(bf16[16,16,128]{2,1,0:T(8,128)(2,1)S(1)} %select.11.kv0), channel_id=1, source_target_pairs={{0,1},{1,2},{2,3},{3,0},{4,5},{5,6},{6,7},{7,4},{8,9},{9,10},{10,1... | collective-permute-start | bytes 196616 | tf_op jit(solution)/shard_map/ppermute | solution.py:380
  53.0 4.8 %collective-permute-start.1 = (bf16[16,16,128]{2,1,0:T(8,128)(2,1)S(1)}, bf16[16,16,128]{2,1,0:T(8,128)(2,1)S(1)}, u32[]{:S(2)}, u32[]{:S(2)}) collective-permute-start(bf16[16,16,128]{2,1,0:T(8,128)(2,1)S(1)} %select.11.kv0), channel_id=1, source_target_pairs={{0,2},{1,3},{2,0},{3,1},{4,6},{5,7},{6,4},{7,5},{8,10},{9,11},{10,... | collective-permute-start | bytes 196616 | tf_op jit(solution)/shard_map/ppermute | solution.py:380
  57.8 2.3 %collective-permute-start.2 = (bf16[16,16,128]{2,1,0:T(8,128)(2,1)S(1)}, bf16[16,16,128]{2,1,0:T(8,128)(2,1)S(1)}, u32[]{:S(2)}, u32[]{:S(2)}) collective-permute-start(bf16[16,16,128]{2,1,0:T(8,128)(2,1)S(1)} %select.11.kv0), channel_id=1, source_target_pairs={{0,3},{1,0},{2,1},{3,2},{4,7},{5,4},{6,5},{7,6},{8,11},{9,8},{10,9... | collective-permute-start | bytes 196616 | tf_op jit(solution)/shard_map/ppermute | solution.py:380
  60.1 0.2 and_select_fusion.bias_ref
  60.3 1.3 %collective-permute-done.1.kv2 = bf16[16,16,128]{2,1,0:T(8,128)(2,1)S(1)} collective-permute-done((bf16[16,16,128]{2,1,0:T(8,128)(2,1)S(1)}, bf16[16,16,128]{2,1,0:T(8,128)(2,1)S(1)}, u32[]{:S(2)}, u32[]{:S(2)}) %collective-permute-start.1) | collective-permute-done | bytes 65568 | tf_op jit(solution)/shard_map/ppermute | solution.py:380
  61.6 1.6 %collective-permute-done.2.kv3 = bf16[16,16,128]{2,1,0:T(8,128)(2,1)S(1)} collective-permute-done((bf16[16,16,128]{2,1,0:T(8,128)(2,1)S(1)}, bf16[16,16,128]{2,1,0:T(8,128)(2,1)S(1)}, u32[]{:S(2)}, u32[]{:S(2)}) %collective-permute-start.2) | collective-permute-done | bytes 65568 | tf_op jit(solution)/shard_map/ppermute | solution.py:380
  63.2 1.9 %early.1 = (bf16[64,16,128]{2,1,0:T(8,128)(2,1)S(1)}, f32[2,128,512]{2,1,0:T(8,128)S(1)}, bf16[2,512,128]{2,1,0:T(8,128)(2,1)S(1)}, f32[512,128]{1,0:T(8,128)S(1)}) custom-call(bf16[64,56,128]{2,1,0:T(8,128)(2,1)S(1)} %all-to-all-done.1.got_ref, bf16[16,16,128]{2,1,0:T(8,128)(2,1)S(1)} %select.11.kv0, bf16[16,16,128]{2,1,0:T(8,128)(2,1)S(1)} %collective-permute-done.kv1, ...), custom_call_target="tpu_custom_call" | custom-call | tf_op jit(solution)/shard_map/early/pallas_call | solution.py:236
  65.1 0.7 copy-done.2
  65.8 1.7 %all-to-all-done.got_ref = bf16[64,32,128]{2,1,0:T(8,128)(2,1)S(1)} async-done(((bf16[64,32,128]{2,1,0:T(8,128)(2,1)}), bf16[64,32,128]{2,1,0:T(8,128)(2,1)S(1)}, u32[]{:S(2)}, u32[]{:S(2)}) %all-to-all-start) | async-done | bytes 524320 | tf_op jit(solution)/shard_map/all_to_all | solution.py:351
  67.5 1.5 %late.1 = (bf16[64,16,128]{2,1,0:T(8,128)(2,1)S(1)}, bf16[4,64,512]{2,1,0:T(8,128)(2,1)S(1)}) custom-call(bf16[64,32,128]{2,1,0:T(8,128)(2,1)S(1)} %all-to-all-done.got_ref, f32[2,128,512]{2,1,0:T(8,128)S(1)} %get-tuple-element.12.sums_ref, bf16[2,512,128]{2,1,0:T(8,128)(2,1)S(1)} %get-tuple-element.13.both_ref, f32[512,128]{1,0:T(8,128)S(1)} %get-tuple-element.14.stat_ref, ...), custom_call_target="tpu_custom_call" | custom-call | tf_op jit(solution)/shard_map/late/pallas_call | solution.py:264
  69.0 10.9 %all_to_all.20.part_ref = bf16[4,64,512]{2,1,0:T(8,128)(2,1)S(1)} all-to-all(bf16[4,64,512]{2,1,0:T(8,128)(2,1)S(1)} %get-tuple-element.15), channel_id=1, replica_groups=mesh['seq'=64,'kvh'=3,'mem'=4] {'mem'}, dimensions={0} | all-to-all | bytes 524288 | tf_op jit(solution)/shard_map/all_to_all | solution.py:351
  79.9 1.6 %spread.1 = bf16[64,48,128]{2,1,0:T(8,128)(2,1)} custom-call(s32[16]{0:T(128)S(1)} %get-tuple-element.24.homes, bf16[4,64,512]{2,1,0:T(8,128)(2,1)S(1)} %all_to_all.20.part_ref, bf16[64,16,128]{2,1,0:T(8,128)(2,1)S(1)} %copy-done.3, bf16[64,16,128]{2,1,0:T(8,128)(2,1)S(1)} %get-tuple-element.17.late_ref), custom_call_target="tpu_custom_call" | custom-call | tf_op jit(solution)/shard_map/spread/pallas_call | solution.py:297
  81.5 10.5 %all-to-all-start.3 = ((bf16[64,48,128]{2,1,0:T(8,128)(2,1)}), bf16[64,48,128]{2,1,0:T(8,128)(2,1)S(1)}, u32[]{:S(2)}, u32[]{:S(2)}) async-start(bf16[64,48,128]{2,1,0:T(8,128)(2,1)} %spread.1), calls=%async_computation.3 | async-start | bytes 1572864 | tf_op jit(solution)/shard_map/all_to_all | solution.py:351
  92.0 23.0 %all-to-all-done.3.got_ref = bf16[64,48,128]{2,1,0:T(8,128)(2,1)S(1)} async-done(((bf16[64,48,128]{2,1,0:T(8,128)(2,1)}), bf16[64,48,128]{2,1,0:T(8,128)(2,1)S(1)}, u32[]{:S(2)}, u32[]{:S(2)}) %all-to-all-start.3) | async-done | bytes 786464 | tf_op jit(solution)/shard_map/all_to_all | solution.py:351
  115.0 1.8 %settle.1 = (bf16[64,8,512]{2,1,0:T(8,128)(2,1)}, f32[32,512]{1,0:T(8,128)}, f32[32,512]{1,0:T(8,128)}) custom-call(s32[64]{0:T(128)S(1)} %dynamic-slice_bitcast_fusion.dest, s32[64]{0:T(128)S(1)} %broadcast_add_fusion.sub, bf16[64,48,128]{2,1,0:T(8,128)(2,1)S(1)} %all-to-all-done.3.got_ref), custom_call_target="tpu_custom_call" | custom-call | tf_op jit(solution)/shard_map/settle/pallas_call | solution.py:331
  (17 shorter events, 0.1 us)
Async XLA Ops:
  3.1 14.8 %copy-start.4 = (s32[64,64]{1,0:T(8,128)S(1)}, s32[64,64]{1,0:T(8,128)}, u32[]{:S(2)}) copy-start(s32[64,64]{1,0:T(8,128)} %dispatch_hbm.1) | copy-start | bytes 49156
  3.2 14.8 %copy-start = (bf16[512,512]{1,0:T(8,128)(2,1)S(1)}, bf16[512,512]{1,0:T(8,128)(2,1)}, u32[]{:S(2)}) copy-start(bf16[512,512]{1,0:T(8,128)(2,1)} %param.9) | copy-start | bytes 1572868
  3.2 14.8 %copy-start.1 = (bf16[512,512]{1,0:T(8,128)(2,1)S(1)}, bf16[512,512]{1,0:T(8,128)(2,1)}, u32[]{:S(2)}) copy-start(bf16[512,512]{1,0:T(8,128)(2,1)} %param.12) | copy-start | bytes 1572868
  3.2 40.3 %all-to-all-start.1 = ((bf16[64,56,128]{2,1,0:T(8,128)(2,1)}), bf16[64,56,128]{2,1,0:T(8,128)(2,1)S(1)}, u32[]{:S(2)}, u32[]{:S(2)}) async-start(bf16[64,56,128]{2,1,0:T(8,128)(2,1)} %first.1), calls=%async_computation.1 | async-start | bytes 1835008 | tf_op jit(solution)/shard_map/all_to_all | solution.py:351
  17.9 1.4 %copy-start.5 = (s32[64,16]{0,1:T(8,128)S(1)}, s32[64,16]{0,1:T(8,128)}, u32[]{:S(2)}) copy-start(s32[64,16]{0,1:T(8,128)} %param.16) | copy-start | bytes 12292
  43.5 6.5 %copy-start.6 = (s32[64,64]{1,0:T(8,128)S(1)}, s32[64,64]{1,0:T(8,128)}, u32[]{:S(2)}) copy-start(s32[64,64]{1,0:T(8,128)} %param.17) | copy-start | bytes 49156
  43.5 24.0 %all-to-all-start = ((bf16[64,32,128]{2,1,0:T(8,128)(2,1)}), bf16[64,32,128]{2,1,0:T(8,128)(2,1)S(1)}, u32[]{:S(2)}, u32[]{:S(2)}) async-start(bf16[64,32,128]{2,1,0:T(8,128)(2,1)} %second.1), calls=%async_computation | async-start | bytes 1048576 | tf_op jit(solution)/shard_map/all_to_all | solution.py:351
  51.1 9.2 %collective-permute-start = (bf16[16,16,128]{2,1,0:T(8,128)(2,1)S(1)}, bf16[16,16,128]{2,1,0:T(8,128)(2,1)S(1)}, u32[]{:S(2)}, u32[]{:S(2)}) collective-permute-start(bf16[16,16,128]{2,1,0:T(8,128)(2,1)S(1)} %select.11.kv0), channel_id=1, source_target_pairs={{0,1},{1,2},{2,3},{3,0},{4,5},{5,6},{6,7},{7,4},{8,9},{9,10},{10,1... | collective-permute-start | bytes 196616 | tf_op jit(solution)/shard_map/ppermute | solution.py:380
  53.0 8.6 %collective-permute-start.1 = (bf16[16,16,128]{2,1,0:T(8,128)(2,1)S(1)}, bf16[16,16,128]{2,1,0:T(8,128)(2,1)S(1)}, u32[]{:S(2)}, u32[]{:S(2)}) collective-permute-start(bf16[16,16,128]{2,1,0:T(8,128)(2,1)S(1)} %select.11.kv0), channel_id=1, source_target_pairs={{0,2},{1,3},{2,0},{3,1},{4,6},{5,7},{6,4},{7,5},{8,10},{9,11},{10,... | collective-permute-start | bytes 196616 | tf_op jit(solution)/shard_map/ppermute | solution.py:380
  57.8 5.3 %collective-permute-start.2 = (bf16[16,16,128]{2,1,0:T(8,128)(2,1)S(1)}, bf16[16,16,128]{2,1,0:T(8,128)(2,1)S(1)}, u32[]{:S(2)}, u32[]{:S(2)}) collective-permute-start(bf16[16,16,128]{2,1,0:T(8,128)(2,1)S(1)} %select.11.kv0), channel_id=1, source_target_pairs={{0,3},{1,0},{2,1},{3,2},{4,7},{5,4},{6,5},{7,6},{8,11},{9,8},{10,9... | collective-permute-start | bytes 196616 | tf_op jit(solution)/shard_map/ppermute | solution.py:380
  65.1 0.7 copy-start.2
  69.0 10.9 %copy-start.3 = (bf16[64,16,128]{2,1,0:T(8,128)(2,1)S(1)}, bf16[64,16,128]{2,1,0:T(8,128)(2,1)}, u32[]{:S(2)}) copy-start(bf16[64,16,128]{2,1,0:T(8,128)(2,1)} %copy-done.2) | copy-start | bytes 786436
  81.5 33.5 %all-to-all-start.3 = ((bf16[64,48,128]{2,1,0:T(8,128)(2,1)}), bf16[64,48,128]{2,1,0:T(8,128)(2,1)S(1)}, u32[]{:S(2)}, u32[]{:S(2)}) async-start(bf16[64,48,128]{2,1,0:T(8,128)(2,1)} %spread.1), calls=%async_computation.3 | async-start | bytes 1572864 | tf_op jit(solution)/shard_map/all_to_all | solution.py:351

commit v3 on v2

--- a/solution.py
+++ b/solution.py
@@ -18,7 +18,7 @@
 HEADS = 4
 TOK = 512
 QROWS = HEADS * SPAN
-HALF = HEADS // 2
+HALF = HEADS
 HROWS = HALF * SPAN
 ROWS_1 = 2 * HROWS + SPAN + 16
 OUT_ROWS = QROWS + 16
@@ -139,39 +139,17 @@
     )(dispatch, listed.T, norm, delta, q, g, k, v)
 
 
-def second_kernel(dest, q_ref, g_ref, out_ref):
-    for j in range(SEQ):
-        slot = dest[j]
-        for h in range(HALF):
-            out_ref[slot, pl.ds(SPAN * h, SPAN), :] = q_ref[j, :, HD * h : HD * h + HD]
-            out_ref[slot, pl.ds(HROWS + SPAN * h, SPAN), :] = g_ref[j, :, HD * h : HD * h + HD]
-
-
-def second(dest, q, g):
-    half = pl.BlockSpec((SEQ, SPAN, HALF * HD), lambda i, d: (0, 0, 1))
-    return pl.pallas_call(
-        second_kernel,
-        out_shape=jax.ShapeDtypeStruct((SEQ, 2 * HROWS, HD), BF),
-        grid_spec=pltpu.PrefetchScalarGridSpec(
-            num_scalar_prefetch=1,
-            grid=(1,),
-            in_specs=[half, half],
-            out_specs=pl.BlockSpec((SEQ, 2 * HROWS, HD), lambda i, d: (0, 0, 0)),
-        ),
-        compiler_params=PARAMS,
-        name="second",
-    )(dest, q, g)
-
-
 def select_kernel(homes, got_ref, out_ref):
     for i in range(NLIST):
-        out_ref[i] = got_ref[homes[i], pl.ds(2 * HROWS + SPAN, 16), :]
+        block = got_ref[homes[i], pl.ds(2 * HROWS + SPAN, 16), :]
+        for m in range(MEM):
+            out_ref[m, i] = block
 
 
 def select(homes, got):
     return pl.pallas_call(
         select_kernel,
-        out_shape=pltpu.VMEM((NLIST, 16, HD), BF),
+        out_shape=jax.ShapeDtypeStruct((MEM, NLIST, 16, HD), BF),
         in_specs=[smem(), vmem()],
         out_specs=vmem(),
         compiler_params=PARAMS,
@@ -187,7 +165,7 @@
         norm = stat[:, i : i + 1] + stat[:, 4 + i : 5 + i]
         delta = stat[:, 8 + i : 9 + i] + stat[:, 12 + i : 13 + i]
         scores = lax.dot_general(q, keys, (((1,), (1,)), ((), ())), preferred_element_type=F32)
-        probs = jnp.exp2(scores * (SCALE * LOG2E) - norm * LOG2E + bias_ref[...])
+        probs = jnp.exp2(scores * (SCALE * LOG2E) - norm * LOG2E + bias_ref[...].astype(F32))
         dprobs = lax.dot_general(g, values, (((1,), (1,)), ((), ())), preferred_element_type=F32)
         dscores = (probs * (dprobs - delta)).astype(BF)
         value_sum += lax.dot_general(g, probs.astype(BF), (((0,), (0,)), ((), ())), preferred_element_type=F32)
@@ -201,58 +179,25 @@
     return lambda h: ref[:, offset + SPAN * h : offset + SPAN * h + SPAN, :].reshape(TOK, HD)
 
 
-def early_kernel(
-    got_ref, kv0, kv1, kv2, kv3, bias_ref, dq_ref, sums_ref, both_ref, stat_ref, key, value,
-):
-    member = lax.axis_index("mem")
+def attend_kernel(got_ref, kv_ref, bias_ref, dq_ref, dkv_ref, key, value, stat_ref):
     lane = lax.broadcasted_iota(jnp.int32, (HD, 2 * HD), 0)
     col = lax.broadcasted_iota(jnp.int32, (HD, 2 * HD), 1)
     for half in range(2):
         total = jnp.zeros((NLIST * 16, 2 * HD), F32)
-        for s, ref in enumerate((kv0, kv1, kv2, kv3)):
-            owner = lax.rem(member + (MEM - s), MEM)
-            source = 64 * half + QUART * (col // HD) + (col % HD) - QUART * owner
-            good = (lane == source) & ((col % HD) // QUART == owner)
+        for m in range(MEM):
+            source = 64 * half + QUART * (col // HD) + (col % HD) - QUART * m
+            good = (lane == source) & ((col % HD) // QUART == m)
             hot = good.astype(F32).astype(BF)
-            total += jnp.dot(ref[...].reshape(NLIST * 16, HD), hot, preferred_element_type=F32)
+            total += jnp.dot(kv_ref[m].reshape(NLIST * 16, HD), hot, preferred_element_type=F32)
         total = total.astype(BF).reshape(NLIST, 16, 2 * HD)
         key[:, 16 * half : 16 * half + 16, :] = total[:, :, :HD]
         value[:, 16 * half : 16 * half + 16, :] = total[:, :, HD:]
     keys = key[...].reshape(TOK, HD)
     values = value[...].reshape(TOK, HD)
-    both_ref[0] = keys
-    both_ref[1] = values
-    stat = got_ref[:, 2 * HROWS : 2 * HROWS + SPAN, :].reshape(TOK, HD).astype(F32)
-    stat_ref[...] = stat
+    stat_ref[...] = got_ref[:, 2 * HROWS : 2 * HROWS + SPAN, :].reshape(TOK, HD).astype(F32)
     zero = jnp.zeros((HD, TOK), F32)
     key_sum, value_sum = heads(
         taker(got_ref, 0), taker(got_ref, HROWS), stat_ref, keys, values, bias_ref, dq_ref, 0, zero, zero
-    )
-    sums_ref[0] = key_sum
-    sums_ref[1] = value_sum
-
-
-def early(got, kvs, bias):
-    return pl.pallas_call(
-        early_kernel,
-        out_shape=(
-            pltpu.VMEM((SEQ, HROWS, HD), BF),
-            pltpu.VMEM((2, HD, TOK), F32),
-            pltpu.VMEM((2, TOK, HD), BF),
-            pltpu.VMEM((TOK, HD), F32),
-        ),
-        in_specs=[vmem()] * 6,
-        out_specs=(vmem(),) * 4,
-        scratch_shapes=[pltpu.VMEM((NLIST, KVCH, HD), BF), pltpu.VMEM((NLIST, KVCH, HD), BF)],
-        compiler_params=PARAMS,
-        name="early",
-    )(got, *kvs, bias)
-
-
-def late_kernel(got_ref, sums_ref, both_ref, stat_ref, bias_ref, dq_ref, dkv_ref):
-    key_sum, value_sum = heads(
-        taker(got_ref, 0), taker(got_ref, HROWS), stat_ref, both_ref[0], both_ref[1], bias_ref, dq_ref, HALF,
-        sums_ref[0], sums_ref[1],
     )
     key_sum = key_sum * SCALE
     for m in range(MEM):
@@ -260,23 +205,27 @@
         dkv_ref[m, QUART : 2 * QUART, :] = value_sum[QUART * m : QUART * m + QUART].astype(BF)
 
 
-def late(got, sums, both, stat, bias):
-    return pl.pallas_call(
-        late_kernel,
+def attend(got, kv, bias):
+    return pl.pallas_call(
+        attend_kernel,
         out_shape=(
-            pltpu.VMEM((SEQ, HROWS, HD), BF),
+            pltpu.VMEM((SEQ, QROWS, HD), BF),
             jax.ShapeDtypeStruct((MEM, 2 * QUART, TOK), BF),
         ),
-        in_specs=[vmem()] * 5,
-        out_specs=(vmem(), vmem()),
+        in_specs=[vmem()] * 3,
+        out_specs=(vmem(),) * 2,
+        scratch_shapes=[
+            pltpu.VMEM((NLIST, KVCH, HD), BF),
+            pltpu.VMEM((NLIST, KVCH, HD), BF),
+            pltpu.VMEM((TOK, HD), F32),
+        ],
         compiler_params=PARAMS,
-        name="late",
-    )(got, sums, both, stat, bias)
-
-
-def spread_kernel(homes, part_ref, early_ref, late_ref, out_ref):
-    out_ref[:, 0:HROWS, :] = early_ref[...]
-    out_ref[:, HROWS:QROWS, :] = late_ref[...]
+        name="attend",
+    )(got, kv, bias)
+
+
+def spread_kernel(homes, part_ref, dq_ref, out_ref):
+    out_ref[:, 0:QROWS, :] = dq_ref[...]
     total = (part_ref[0].astype(F32) + part_ref[1].astype(F32)) + (
         part_ref[2].astype(F32) + part_ref[3].astype(F32)
     )
@@ -293,15 +242,15 @@
         out_ref[homes[i], pl.ds(QROWS, 16), :] = block.astype(BF)
 
 
-def spread(homes, part, dq_early, dq_late):
+def spread(homes, part, dq):
     return pl.pallas_call(
         spread_kernel,
         out_shape=jax.ShapeDtypeStruct((SEQ, OUT_ROWS, HD), BF),
-        in_specs=[smem(), vmem(), vmem(), vmem()],
+        in_specs=[smem(), vmem(), vmem()],
         out_specs=vmem(),
         compiler_params=PARAMS,
         name="spread",
-    )(homes, part, dq_early, dq_late)
+    )(homes, part, dq)
 
 
 def settle_kernel(dest, sub, got_ref, dq_ref, dk_ref, dv_ref, acc):
@@ -362,7 +311,6 @@
     dest = lax.dynamic_index_in_dim(dispatch, home, 0, keepdims=False)
     at_home = listed_spans // NLIST == home
     sub = jnp.sum(jnp.where(at_home, listed_spans % NLIST - NLIST, 0), axis=1) + NLIST
-    got_2 = exchanged(second(dest, q, g), "seq")
     my_list = lax.dynamic_index_in_dim(listed_spans, home, 0, keepdims=False)
     homes = my_list // NLIST
     here = dispatch == home
@@ -373,17 +321,13 @@
     lowest = jnp.repeat(starts, SPAN)
     key_pos = (my_list[:, None] * KVCH + jnp.arange(KVCH, dtype=jnp.int32)[None, :]).reshape(-1)
     allowed = (key_pos[None, :] <= query_pos[:, None]) & (key_pos[None, :] >= lowest[:, None])
-    bias = jnp.where(allowed, 0.0, -1e30).astype(F32)
-
-    chosen = near(select(homes, got_1))
-    kvs = [chosen] + [
-        near(lax.ppermute(chosen, "mem", [(i, (i + s) % MEM) for i in range(MEM)])) for s in range(1, MEM)
-    ]
-    bias = near(bias)
-    dq_early, sums, both, stat = map(near, early(got_1, kvs, bias))
-    dq_late, dkv = late(got_2, sums, both, stat, bias)
+    bias = jnp.where(allowed, 0.0, -1e30).astype(BF)
+
+    chosen = select(homes, got_1)
+    kv = exchanged(chosen, "mem")
+    dq, dkv = attend(got_1, kv, near(bias))
     part = exchanged(dkv, "mem")
-    back = exchanged(spread(homes, part, dq_early, near(dq_late)), "seq")
+    back = exchanged(spread(homes, part, near(dq)), "seq")
     dq_out, dk_out, dv_out = settle(dest, sub, back)
     return dq_out.reshape(TOK, HEADS * HD), dk_out, dv_out
 

time: 117 us -> 116 us (level)
  starting transfers between devices: 40.5 us -> 28 us
  waiting for transfers between devices: 51.5 us -> 64 us
    all_to_all x3, waiting for transfers between devices: 48.6 us -> 64 us  [exchanged(): lax.all_to_all(value, axis, split_axis=0, concat_axis=0, tiled=True)]
    ppermute x3 -> x0, starting transfers between devices: 9 us -> none  [local(): lax.ppermute(chosen, 'mem', [(i, (i + s) % MEM) for i in range(MEM)])]
    all_to_all x3, starting transfers between devices: 31.5 us -> 28 us  [exchanged(): lax.all_to_all(value, axis, split_axis=0, concat_axis=0, tiled=True)]
    ppermute x3 -> x0, waiting for transfers between devices: 2.82 us -> none  [local(): lax.ppermute(chosen, 'mem', [(i, (i + s) % MEM) for i in range(MEM)])]
    pallas_call x4 -> x2, Pallas kernels: 5.4 us -> 4.3 us  [the longest x1 3.02 us: attend(): pl.pallas_call(attend_kernel, out_shape=(pltpu.VMEM((SEQ, QROWS, HD), BF)...]
  transfers between devices with their start and end apart: 6 -> 3, of which waited for: 5 -> 3; matrix products, arithmetic and copies ran while one was open for 1% -> 1% of each run, Pallas kernels for 3% -> 0%
where the time goes in v3:
time: 116 us; the launch traced here: 115 us
  waiting for transfers between devices  64 us (55%)
  starting transfers between devices  28 us (24%)
  blocking collectives  11 us (9%)
  Pallas kernels  10.5 us (9%)
    all_to_all x3, waiting for transfers between devices, exchanged(): lax.all_to_all(value, axis, split_axis=0, concat_axis=0, tiled=True)  64 us
    all_to_all x3, starting transfers between devices, exchanged(): lax.all_to_all(value, axis, split_axis=0, concat_axis=0, tiled=True)  28 us
    all_to_all x1, blocking collectives, exchanged(): lax.all_to_all(value, axis, split_axis=0, concat_axis=0, tiled=True)  11 us
    pallas_call x1, Pallas kernels, attend(): pl.pallas_call(attend_kernel, out_shape=(pltpu.VMEM((SEQ, QROWS, HD), BF)...  3.02 us
    pallas_call x1, Pallas kernels, first(): pl.pallas_call(first_kernel, out_shape=jax.ShapeDtypeStruct((SEQ, ROWS_1,...  2.75 us
  transfers between devices with their start and end apart: 3, of which 3 were waited for; matrix products, arithmetic and copies ran while one was open for 1% of the time, Pallas kernels for 0%

profile of v3, /device:TPU:1, one launch (start us, length us, event | category | flops | bytes accessed | tf_op | source)
XLA Modules:
  0.0 115.4 jit_solution(5845757172336109883)
XLA Ops:
  0.6 2.8 %first.1 = bf16[64,88,128]{2,1,0:T(8,128)(2,1)} custom-call(s32[64,64]{1,0:T(8,128)} %dispatch_hbm.1, s32[16,64]{1,0:T(8,128)} %bitcast.8, f32[4,512]{1,0:T(4,128)} %norm_hbm.1, f32[4,512]{1,0:T(4,128)} %delta_hbm.1, bf16[64,8,512]{2,1,0:T(8,128)(2,1)} %bitcast.6, bf16[64,8,512]{2,1,0:T(8,128)(2,1)} %bitcast.7, bf16[512,384]{1,0:T(8,128)(2,1)} %k_hbm.1, ...), custom_call_target="tpu_custom_call" | custom-call | tf_op jit(solution)/shard_map/first/pallas_call | solution.py:117
  3.4 0.0 copy-start.1
  3.4 0.0 copy-start
  3.4 0.0 copy-start.2
  3.4 14.7 %all-to-all-start = ((bf16[64,88,128]{2,1,0:T(8,128)(2,1)}), bf16[64,88,128]{2,1,0:T(8,128)(2,1)S(1)}, u32[]{:S(2)}, u32[]{:S(2)}) async-start(bf16[64,88,128]{2,1,0:T(8,128)(2,1)} %first.1), calls=%async_computation | async-start | bytes 2883584 | tf_op jit(solution)/shard_map/all_to_all | solution.py:300
  18.2 0.0 copy-done.1
  18.2 0.2 dynamic-slice_reduce_fusion
  18.4 0.1 iota_add_fusion.1
  18.4 0.1 add.81
  18.5 0.0 copy-done
  18.5 0.0 copy-done.2
  18.5 0.2 select_reduce_fusion.1
  18.7 0.1 broadcast_in_dim.25
  18.8 0.1 ge.6
  18.9 35.8 %all-to-all-done.got_ref = bf16[64,88,128]{2,1,0:T(8,128)(2,1)S(1)} async-done(((bf16[64,88,128]{2,1,0:T(8,128)(2,1)}), bf16[64,88,128]{2,1,0:T(8,128)(2,1)S(1)}, u32[]{:S(2)}, u32[]{:S(2)}) %all-to-all-start) | async-done | bytes 1441824 | tf_op jit(solution)/shard_map/all_to_all | solution.py:300
  54.6 1.3 %select.11 = bf16[4,16,16,128]{3,2,1,0:T(8,128)(2,1)} custom-call(s32[16]{0:T(128)S(1)} %get-tuple-element.16.homes, bf16[64,88,128]{2,1,0:T(8,128)(2,1)S(1)} %all-to-all-done.got_ref), custom_call_target="tpu_custom_call" | custom-call | tf_op jit(solution)/shard_map/select/pallas_call | solution.py:150
  55.9 3.9 %all-to-all-start.1 = ((bf16[4,16,16,128]{3,2,1,0:T(8,128)(2,1)}), bf16[4,16,16,128]{3,2,1,0:T(8,128)(2,1)S(1)}, u32[]{:S(2)}, u32[]{:S(2)}) async-start(bf16[4,16,16,128]{3,2,1,0:T(8,128)(2,1)} %select.11), calls=%async_computation.1 | async-start | bytes 524288 | tf_op jit(solution)/shard_map/all_to_all | solution.py:300
  59.8 0.1 iota_add_fusion
  59.9 0.1 add.88
  60.0 0.2 select_convert_fusion.bias_ref
  60.3 5.3 %all-to-all-done.1.kv_ref = bf16[4,16,16,128]{3,2,1,0:T(8,128)(2,1)S(1)} async-done(((bf16[4,16,16,128]{3,2,1,0:T(8,128)(2,1)}), bf16[4,16,16,128]{3,2,1,0:T(8,128)(2,1)S(1)}, u32[]{:S(2)}, u32[]{:S(2)}) %all-to-all-start.1) | async-done | bytes 262176 | tf_op jit(solution)/shard_map/all_to_all | solution.py:300
  65.6 3.0 %attend.1 = (bf16[64,32,128]{2,1,0:T(8,128)(2,1)S(1)}, bf16[4,64,512]{2,1,0:T(8,128)(2,1)S(1)}) custom-call(bf16[64,88,128]{2,1,0:T(8,128)(2,1)S(1)} %all-to-all-done.got_ref, bf16[4,16,16,128]{3,2,1,0:T(8,128)(2,1)S(1)} %all-to-all-done.1.kv_ref, bf16[512,512]{1,0:T(8,128)(2,1)S(1)} %select_convert_fusion.bias_ref), custom_call_target="tpu_custom_call" | custom-call | tf_op jit(solution)/shard_map/attend/pallas_call | solution.py:209
  68.6 11.0 %all_to_all.20.part_ref = bf16[4,64,512]{2,1,0:T(8,128)(2,1)S(1)} all-to-all(bf16[4,64,512]{2,1,0:T(8,128)(2,1)S(1)} %get-tuple-element.8), channel_id=1, replica_groups=mesh['seq'=64,'kvh'=3,'mem'=4] {'mem'}, dimensions={0} | all-to-all | bytes 524288 | tf_op jit(solution)/shard_map/all_to_all | solution.py:300
  79.6 1.6 %spread.1 = bf16[64,48,128]{2,1,0:T(8,128)(2,1)} custom-call(s32[16]{0:T(128)S(1)} %get-tuple-element.16.homes, bf16[4,64,512]{2,1,0:T(8,128)(2,1)S(1)} %all_to_all.20.part_ref, bf16[64,32,128]{2,1,0:T(8,128)(2,1)S(1)} %get-tuple-element.9.dq_ref), custom_call_target="tpu_custom_call" | custom-call | tf_op jit(solution)/shard_map/spread/pallas_call | solution.py:246
  81.2 9.3 %all-to-all-start.3 = ((bf16[64,48,128]{2,1,0:T(8,128)(2,1)}), bf16[64,48,128]{2,1,0:T(8,128)(2,1)S(1)}, u32[]{:S(2)}, u32[]{:S(2)}) async-start(bf16[64,48,128]{2,1,0:T(8,128)(2,1)} %spread.1), calls=%async_computation.3 | async-start | bytes 1572864 | tf_op jit(solution)/shard_map/all_to_all | solution.py:300
  90.6 22.9 %all-to-all-done.3.got_ref = bf16[64,48,128]{2,1,0:T(8,128)(2,1)S(1)} async-done(((bf16[64,48,128]{2,1,0:T(8,128)(2,1)}), bf16[64,48,128]{2,1,0:T(8,128)(2,1)S(1)}, u32[]{:S(2)}, u32[]{:S(2)}) %all-to-all-start.3) | async-done | bytes 786464 | tf_op jit(solution)/shard_map/all_to_all | solution.py:300
  113.5 1.9 %settle.1 = (bf16[64,8,512]{2,1,0:T(8,128)(2,1)}, f32[32,512]{1,0:T(8,128)}, f32[32,512]{1,0:T(8,128)}) custom-call(s32[64]{0:T(128)S(1)} %dynamic-slice_bitcast_fusion.dest, s32[64]{0:T(128)S(1)} %broadcast_add_fusion.sub, bf16[64,48,128]{2,1,0:T(8,128)(2,1)S(1)} %all-to-all-done.3.got_ref), custom_call_target="tpu_custom_call" | custom-call | tf_op jit(solution)/shard_map/settle/pallas_call | solution.py:280
  (6 shorter events, 0.1 us)
Async XLA Ops:
  3.4 14.8 %copy-start.1 = (s32[64,16]{0,1:T(8,128)S(1)}, s32[64,16]{0,1:T(8,128)}, u32[]{:S(2)}) copy-start(s32[64,16]{0,1:T(8,128)} %param.16) | copy-start | bytes 12292
  3.4 15.1 %copy-start = (s32[64,64]{1,0:T(8,128)S(1)}, s32[64,64]{1,0:T(8,128)}, u32[]{:S(2)}) copy-start(s32[64,64]{1,0:T(8,128)} %dispatch_hbm.1) | copy-start | bytes 49156
  3.4 15.1 %copy-start.2 = (s32[64,64]{1,0:T(8,128)S(1)}, s32[64,64]{1,0:T(8,128)}, u32[]{:S(2)}) copy-start(s32[64,64]{1,0:T(8,128)} %param.17) | copy-start | bytes 49156
  3.4 51.2 %all-to-all-start = ((bf16[64,88,128]{2,1,0:T(8,128)(2,1)}), bf16[64,88,128]{2,1,0:T(8,128)(2,1)S(1)}, u32[]{:S(2)}, u32[]{:S(2)}) async-start(bf16[64,88,128]{2,1,0:T(8,128)(2,1)} %first.1), calls=%async_computation | async-start | bytes 2883584 | tf_op jit(solution)/shard_map/all_to_all | solution.py:300
  55.9 9.6 %all-to-all-start.1 = ((bf16[4,16,16,128]{3,2,1,0:T(8,128)(2,1)}), bf16[4,16,16,128]{3,2,1,0:T(8,128)(2,1)S(1)}, u32[]{:S(2)}, u32[]{:S(2)}) async-start(bf16[4,16,16,128]{3,2,1,0:T(8,128)(2,1)} %select.11), calls=%async_computation.1 | async-start | bytes 524288 | tf_op jit(solution)/shard_map/all_to_all | solution.py:300
  81.2 32.4 %all-to-all-start.3 = ((bf16[64,48,128]{2,1,0:T(8,128)(2,1)}), bf16[64,48,128]{2,1,0:T(8,128)(2,1)S(1)}, u32[]{:S(2)}, u32[]{:S(2)}) async-start(bf16[64,48,128]{2,1,0:T(8,128)(2,1)} %spread.1), calls=%async_computation.3 | async-start | bytes 1572864 | tf_op jit(solution)/shard_map/all_to_all | solution.py:300

commit v4 on v3

--- a/solution.py
+++ b/solution.py
@@ -149,7 +149,7 @@
 def select(homes, got):
     return pl.pallas_call(
         select_kernel,
-        out_shape=jax.ShapeDtypeStruct((MEM, NLIST, 16, HD), BF),
+        out_shape=pltpu.VMEM((MEM, NLIST, 16, HD), BF),
         in_specs=[smem(), vmem()],
         out_specs=vmem(),
         compiler_params=PARAMS,
@@ -253,15 +253,18 @@
     )(homes, part, dq)
 
 
-def settle_kernel(dest, sub, got_ref, dq_ref, dk_ref, dv_ref, acc):
-    acc[...] = jnp.zeros_like(acc)
+def settle_kernel(dest, sub, got_ref, dq_ref, dk_ref, dv_ref, acc, *others):
+    parts = (acc, *others)
+    for part in parts:
+        part[...] = jnp.zeros_like(part)
     for j in range(SEQ):
         slot = dest[j]
         for h in range(HEADS):
             dq_ref[j, :, HD * h : HD * h + HD] = got_ref[slot, pl.ds(SPAN * h, SPAN), :]
 
     for n in range(SEQ):
-        acc[sub[n]] += got_ref[n, pl.ds(QROWS, 16), :].astype(F32)
+        parts[n % len(parts)][sub[n]] += got_ref[n, pl.ds(QROWS, 16), :].astype(F32)
+    acc[...] = (parts[0][...] + parts[1][...]) + (parts[2][...] + parts[3][...])
     lane = lax.broadcasted_iota(jnp.int32, (16, HD), 1) // KVCH
     for ref, first in ((dk_ref, 0), (dv_ref, 2)):
         for b in range(2):
@@ -286,7 +289,7 @@
         ),
         in_specs=[smem(), smem(), vmem()],
         out_specs=(vmem(), vmem(), vmem()),
-        scratch_shapes=[pltpu.VMEM((NLIST + 1, 16, HD), F32)],
+        scratch_shapes=[pltpu.VMEM((NLIST + 1, 16, HD), F32)] * 4,
         compiler_params=PARAMS,
         name="settle",
     )(dest, sub, got)

time: 116 us -> 116 us (level)
  no operation moved by 1% of the time
where the time goes in v4:
time: 116 us; the launch traced here: 115 us
  waiting for transfers between devices  64 us (55%)
  starting transfers between devices  28 us (24%)
  blocking collectives  11 us (9%)
  Pallas kernels  10.2 us (9%)
    all_to_all x3, waiting for transfers between devices, exchanged(): lax.all_to_all(value, axis, split_axis=0, concat_axis=0, tiled=True)  64 us
    all_to_all x3, starting transfers between devices, exchanged(): lax.all_to_all(value, axis, split_axis=0, concat_axis=0, tiled=True)  28 us
    all_to_all x1, blocking collectives, exchanged(): lax.all_to_all(value, axis, split_axis=0, concat_axis=0, tiled=True)  11 us
    pallas_call x1, Pallas kernels, attend(): pl.pallas_call(attend_kernel, out_shape=(pltpu.VMEM((SEQ, QROWS, HD), BF)...  3.02 us
    pallas_call x1, Pallas kernels, first(): pl.pallas_call(first_kernel, out_shape=jax.ShapeDtypeStruct((SEQ, ROWS_1,...  2.75 us
  transfers between devices with their start and end apart: 3, of which 3 were waited for; matrix products, arithmetic and copies ran while one was open for 1% of the time, Pallas kernels for 0%

profile of v4, /device:TPU:1, one launch (start us, length us, event | category | flops | bytes accessed | tf_op | source)
XLA Modules:
  0.0 115.2 jit_solution(1975779610207756584)
XLA Ops:
  0.6 2.8 %first.1 = bf16[64,88,128]{2,1,0:T(8,128)(2,1)} custom-call(s32[64,64]{1,0:T(8,128)} %dispatch_hbm.1, s32[16,64]{1,0:T(8,128)} %bitcast.8, f32[4,512]{1,0:T(4,128)} %norm_hbm.1, f32[4,512]{1,0:T(4,128)} %delta_hbm.1, bf16[64,8,512]{2,1,0:T(8,128)(2,1)} %bitcast.6, bf16[64,8,512]{2,1,0:T(8,128)(2,1)} %bitcast.7, bf16[512,384]{1,0:T(8,128)(2,1)} %k_hbm.1, ...), custom_call_target="tpu_custom_call" | custom-call | tf_op jit(solution)/shard_map/first/pallas_call | solution.py:117
  3.4 0.0 copy-start.1
  3.4 0.0 copy-start
  3.4 0.0 copy-start.2
  3.4 14.7 %all-to-all-start = ((bf16[64,88,128]{2,1,0:T(8,128)(2,1)}), bf16[64,88,128]{2,1,0:T(8,128)(2,1)S(1)}, u32[]{:S(2)}, u32[]{:S(2)}) async-start(bf16[64,88,128]{2,1,0:T(8,128)(2,1)} %first.1), calls=%async_computation | async-start | bytes 2883584 | tf_op jit(solution)/shard_map/all_to_all | solution.py:303
  18.2 0.0 copy-done.1
  18.2 0.2 dynamic-slice_reduce_fusion
  18.4 0.1 iota_add_fusion.1
  18.4 0.1 add.81
  18.5 0.0 copy-done
  18.5 0.0 copy-done.2
  18.5 0.2 select_reduce_fusion.1
  18.7 0.1 broadcast_in_dim.25
  18.8 0.1 ge.6
  18.9 35.8 %all-to-all-done.got_ref = bf16[64,88,128]{2,1,0:T(8,128)(2,1)S(1)} async-done(((bf16[64,88,128]{2,1,0:T(8,128)(2,1)}), bf16[64,88,128]{2,1,0:T(8,128)(2,1)S(1)}, u32[]{:S(2)}, u32[]{:S(2)}) %all-to-all-start) | async-done | bytes 1441824 | tf_op jit(solution)/shard_map/all_to_all | solution.py:303
  54.6 1.3 %select.11 = bf16[4,16,16,128]{3,2,1,0:T(8,128)(2,1)} custom-call(s32[16]{0:T(128)S(1)} %get-tuple-element.16.homes, bf16[64,88,128]{2,1,0:T(8,128)(2,1)S(1)} %all-to-all-done.got_ref), custom_call_target="tpu_custom_call" | custom-call | tf_op jit(solution)/shard_map/select/pallas_call | solution.py:150
  55.9 3.9 %all-to-all-start.1 = ((bf16[4,16,16,128]{3,2,1,0:T(8,128)(2,1)}), bf16[4,16,16,128]{3,2,1,0:T(8,128)(2,1)S(1)}, u32[]{:S(2)}, u32[]{:S(2)}) async-start(bf16[4,16,16,128]{3,2,1,0:T(8,128)(2,1)} %select.11), calls=%async_computation.1 | async-start | bytes 524288 | tf_op jit(solution)/shard_map/all_to_all | solution.py:303
  59.8 0.1 iota_add_fusion
  59.9 0.1 add.88
  60.0 0.2 select_convert_fusion.bias_ref
  60.2 5.3 %all-to-all-done.1.kv_ref = bf16[4,16,16,128]{3,2,1,0:T(8,128)(2,1)S(1)} async-done(((bf16[4,16,16,128]{3,2,1,0:T(8,128)(2,1)}), bf16[4,16,16,128]{3,2,1,0:T(8,128)(2,1)S(1)}, u32[]{:S(2)}, u32[]{:S(2)}) %all-to-all-start.1) | async-done | bytes 262176 | tf_op jit(solution)/shard_map/all_to_all | solution.py:303
  65.6 3.0 %attend.1 = (bf16[64,32,128]{2,1,0:T(8,128)(2,1)S(1)}, bf16[4,64,512]{2,1,0:T(8,128)(2,1)S(1)}) custom-call(bf16[64,88,128]{2,1,0:T(8,128)(2,1)S(1)} %all-to-all-done.got_ref, bf16[4,16,16,128]{3,2,1,0:T(8,128)(2,1)S(1)} %all-to-all-done.1.kv_ref, bf16[512,512]{1,0:T(8,128)(2,1)S(1)} %select_convert_fusion.bias_ref), custom_call_target="tpu_custom_call" | custom-call | tf_op jit(solution)/shard_map/attend/pallas_call | solution.py:209
  68.6 11.0 %all_to_all.20.part_ref = bf16[4,64,512]{2,1,0:T(8,128)(2,1)S(1)} all-to-all(bf16[4,64,512]{2,1,0:T(8,128)(2,1)S(1)} %get-tuple-element.8), channel_id=1, replica_groups=mesh['seq'=64,'kvh'=3,'mem'=4] {'mem'}, dimensions={0} | all-to-all | bytes 524288 | tf_op jit(solution)/shard_map/all_to_all | solution.py:303
  79.6 1.6 %spread.1 = bf16[64,48,128]{2,1,0:T(8,128)(2,1)} custom-call(s32[16]{0:T(128)S(1)} %get-tuple-element.16.homes, bf16[4,64,512]{2,1,0:T(8,128)(2,1)S(1)} %all_to_all.20.part_ref, bf16[64,32,128]{2,1,0:T(8,128)(2,1)S(1)} %get-tuple-element.9.dq_ref), custom_call_target="tpu_custom_call" | custom-call | tf_op jit(solution)/shard_map/spread/pallas_call | solution.py:246
  81.2 9.3 %all-to-all-start.3 = ((bf16[64,48,128]{2,1,0:T(8,128)(2,1)}), bf16[64,48,128]{2,1,0:T(8,128)(2,1)S(1)}, u32[]{:S(2)}, u32[]{:S(2)}) async-start(bf16[64,48,128]{2,1,0:T(8,128)(2,1)} %spread.1), calls=%async_computation.3 | async-start | bytes 1572864 | tf_op jit(solution)/shard_map/all_to_all | solution.py:303
  90.6 22.9 %all-to-all-done.3.got_ref = bf16[64,48,128]{2,1,0:T(8,128)(2,1)S(1)} async-done(((bf16[64,48,128]{2,1,0:T(8,128)(2,1)}), bf16[64,48,128]{2,1,0:T(8,128)(2,1)S(1)}, u32[]{:S(2)}, u32[]{:S(2)}) %all-to-all-start.3) | async-done | bytes 786464 | tf_op jit(solution)/shard_map/all_to_all | solution.py:303
  113.5 1.6 %settle.1 = (bf16[64,8,512]{2,1,0:T(8,128)(2,1)}, f32[32,512]{1,0:T(8,128)}, f32[32,512]{1,0:T(8,128)}) custom-call(s32[64]{0:T(128)S(1)} %dynamic-slice_bitcast_fusion.dest, s32[64]{0:T(128)S(1)} %broadcast_add_fusion.sub, bf16[64,48,128]{2,1,0:T(8,128)(2,1)S(1)} %all-to-all-done.3.got_ref), custom_call_target="tpu_custom_call" | custom-call | tf_op jit(solution)/shard_map/settle/pallas_call | solution.py:283
  (6 shorter events, 0.1 us)
Async XLA Ops:
  3.4 14.8 %copy-start.1 = (s32[64,16]{0,1:T(8,128)S(1)}, s32[64,16]{0,1:T(8,128)}, u32[]{:S(2)}) copy-start(s32[64,16]{0,1:T(8,128)} %param.16) | copy-start | bytes 12292
  3.4 15.1 %copy-start = (s32[64,64]{1,0:T(8,128)S(1)}, s32[64,64]{1,0:T(8,128)}, u32[]{:S(2)}) copy-start(s32[64,64]{1,0:T(8,128)} %dispatch_hbm.1) | copy-start | bytes 49156
  3.4 15.1 %copy-start.2 = (s32[64,64]{1,0:T(8,128)S(1)}, s32[64,64]{1,0:T(8,128)}, u32[]{:S(2)}) copy-start(s32[64,64]{1,0:T(8,128)} %param.17) | copy-start | bytes 49156
  3.4 51.2 %all-to-all-start = ((bf16[64,88,128]{2,1,0:T(8,128)(2,1)}), bf16[64,88,128]{2,1,0:T(8,128)(2,1)S(1)}, u32[]{:S(2)}, u32[]{:S(2)}) async-start(bf16[64,88,128]{2,1,0:T(8,128)(2,1)} %first.1), calls=%async_computation | async-start | bytes 2883584 | tf_op jit(solution)/shard_map/all_to_all | solution.py:303
  55.9 9.6 %all-to-all-start.1 = ((bf16[4,16,16,128]{3,2,1,0:T(8,128)(2,1)}), bf16[4,16,16,128]{3,2,1,0:T(8,128)(2,1)S(1)}, u32[]{:S(2)}, u32[]{:S(2)}) async-start(bf16[4,16,16,128]{3,2,1,0:T(8,128)(2,1)} %select.11), calls=%async_computation.1 | async-start | bytes 524288 | tf_op jit(solution)/shard_map/all_to_all | solution.py:303
  81.2 32.4 %all-to-all-start.3 = ((bf16[64,48,128]{2,1,0:T(8,128)(2,1)}), bf16[64,48,128]{2,1,0:T(8,128)(2,1)S(1)}, u32[]{:S(2)}, u32[]{:S(2)}) async-start(bf16[64,48,128]{2,1,0:T(8,128)(2,1)} %spread.1), calls=%async_computation.3 | async-start | bytes 1572864 | tf_op jit(solution)/shard_map/all_to_all | solution.py:303
